TPU v7x, 128 devices: a whole 4x4x4 slice. The times are simulated.
128 devices in a mesh: group: 8 (over x, y_hi), member: 16 (over y_lo, z, core).
Axes of the slice: x: 4, y: 4 (y_hi: 2, y_lo: 2; y = y_hi * 2 + y_lo), z: 4, core: 2. Of those that a mesh axis runs over, the one named last changes fastest.
Arguments:
- factors: bfloat16 [8, 8192, 8192], P('group', 'member'), as said below
- owner: int32 [1], replicated, may hold values from 0 to 7
- grads: bfloat16 [8192, 1024], P(None, 'group')
Outputs:
- new_factor: bfloat16 [8192, 8192], P('member', 'group')
Inputs may be any that keep to these rules, and one draw needn't show every extreme that they name: `owner`: index of the group that owns the updated factor. `factors`: every group's factor is upper triangular with a positive diagonal.
All inputs are finite; a program needn't handle non-finite values.
Results may differ from a plain program's by a relative error of at most 0.0061.
Values may be sent and summed in bfloat16 or wider, within the bound.
No kernel may reach another device: no remote copies, remote signals or barrier semaphores. Data moves between devices by JAX's collectives and lax.ppermute only.
A program may use at most 192 MiB of HBM per device.

v0:
```python
import jax
import jax.numpy as jnp
from jax import lax
from jax.sharding import Mesh
from jax.sharding import PartitionSpec as P

MEMBER = ("member_0", "member_1", "member_2")
GROUP_MEMBER = ("group", "member_0", "member_1", "member_2")


step_size = 1.0
highest = lax.Precision.HIGHEST


def padded_to(lines, peers):
    spare = -len(lines) % peers
    return jnp.pad(lines, [(0, spare)] + [(0, 0)] * (lines.ndim - 1))


def broadcast_by_parts(value, axis, root):
    lines = jnp.where(lax.axis_index(axis) == root, value, jnp.zeros_like(value)).reshape(
        -1, *value.shape[1:][-1:]
    )
    padded = padded_to(lines, lax.axis_size(axis))
    own = lax.psum_scatter(padded, axis, scatter_dimension=0, tiled=True)
    return lax.all_gather(own, axis, axis=0, tiled=True)[: len(lines)].reshape(value.shape)


def cut_along(value, dim, peers):
    before, after = (value.shape[:dim], value.shape[dim + 1 :])
    return jnp.moveaxis(value.reshape(*before, peers, -1, *after), dim, 0)


def sum_at_owner(value, axis, dim):
    peers = lax.axis_size(axis)
    tiles = lax.all_to_all(cut_along(value, dim, peers), axis, 0, 0, tiled=True)
    return jnp.sum(tiles, axis=0)


def in_order(tiles, dim):
    tiles = jnp.moveaxis(tiles, 0, dim)
    dims = tiles.shape
    return tiles.reshape(*dims[:dim], dims[dim] * dims[dim + 1], *dims[dim + 2 :])


def sent_to_all(value, axis):
    copies = jnp.broadcast_to(value, (lax.axis_size(axis), *value.shape))
    return lax.all_to_all(copies, axis, split_axis=0, concat_axis=0, tiled=True)


def gathered_copies(value, axis, dim):
    return in_order(sent_to_all(value, axis), dim)


def nothing_yet(value, identity):
    return jnp.broadcast_to(jnp.asarray(identity, value.dtype), value.shape)


def prefix_by_axis(value, axes, combine, identity):
    before = start = nothing_yet(value, identity)
    total = value
    for axis in reversed(axes):
        peers, index = (lax.axis_size(axis), lax.axis_index(axis))
        pieces = lax.all_gather(total, axis)
        inside, total = (start, start)
        for k in reversed(range(peers)):
            passed = k > index
            total = combine(total, pieces[k])
            inside = jnp.where(passed, total, inside)
        before = combine(inside, before)
    return before


def contract_rows(left_block, right_block):
    return lax.dot_general(
        left_block, right_block, (((0,), (0,)), ((), ())), preferred_element_type=jnp.float32
    )


def add_blocks(earlier_sum, later_sum):
    return earlier_sum + later_sum


def shards(factors, owner, grads):
    local_panel = factors[0]
    factor_panel = broadcast_by_parts(local_panel, "group", owner[0])
    projected = jnp.dot(factor_panel, grads, preferred_element_type=jnp.float32).astype(
        jnp.bfloat16
    )
    precond = sum_at_owner(contract_rows(factor_panel, projected), MEMBER, 0).astype(jnp.bfloat16)
    precond_wide = precond.astype(jnp.float32)
    square_total = lax.psum(jnp.sum(precond_wide * precond_wide), GROUP_MEMBER)
    factor_order = factor_panel.shape[1]
    group_count = lax.axis_size("group")
    total_columns = precond.shape[1] * group_count
    mean_square = square_total / (factor_order * total_columns)
    step_rate = step_size / (1.0 + mean_square)
    block_width = factor_order // group_count
    group_index = lax.axis_index("group")
    own_block = lax.dynamic_slice_in_dim(factor_panel, group_index * block_width, block_width, 1)
    left_rows = gathered_copies(precond, "group", 1)
    partial_terms = contract_rows(left_rows, own_block)
    tail_total = prefix_by_axis(partial_terms, MEMBER, add_blocks, jnp.zeros_like(partial_terms))
    diagonal_gram = jnp.triu(jnp.dot(left_rows, left_rows.T, preferred_element_type=jnp.float32))
    combined = jnp.dot(left_rows.astype(jnp.float32), tail_total, precision=highest)
    combined = combined + jnp.dot(diagonal_gram, own_block.astype(jnp.float32), precision=highest)
    updated = (1.0 + step_rate) * own_block.astype(
        jnp.float32
    ) - step_rate / total_columns * combined
    return updated.astype(jnp.bfloat16)


def solution(mesh):
    split = Mesh(
        mesh.devices.reshape(mesh.shape["group"], 2, 4, 2),
        ("group", "member_0", "member_1", "member_2"),
    )
    in_specs = (P("group", MEMBER, None), P(), P(None, "group"))
    out_specs = P(MEMBER, "group")
    return jax.shard_map(
        shards, mesh=split, in_specs=in_specs, out_specs=out_specs, check_vma=False
    )
```

profile of v0, /device:TPU:1, one launch (start us, length us, event | category | flops | bytes accessed | tf_op | source)
XLA Modules:
  0.0 656.9 jit_solution(9988132946550766310)
XLA Ops:
  7.3 3.8 select_bitcast_fusion
  11.2 120.8 %reduce-scatter.2.cloned.1.call-done = bf16[64,8192]{1,0:T(8,128)(2,1)} async-done(((bf16[512,8192]{1,0:T(8,128)(2,1)}), bf16[64,8192]{1,0:T(8,128)(2,1)}) %reduce-scatter.2.cloned.1.call-update) | async-done | bytes 1048592 | tf_op jit(solution)/shard_map/reduce_scatter | solution.py:25
  132.0 109.2 %all-gather.7.cloned.1.call-done = bf16[512,8192]{1,0:T(8,128)(2,1)} async-done(((bf16[64,8192]{1,0:T(8,128)(2,1)}), bf16[512,8192]{1,0:T(8,128)(2,1)}) %all-gather.7.cloned.1.call-update) | async-done | bytes 8388624 | tf_op jit(solution)/shard_map/all_gather | solution.py:26
  241.3 5.9 convolution_convert_fusion
  247.1 2.4 fusion.33
  249.5 54.6 %all_to_all.10 = f32[16,512,128]{2,1,0:T(8,128)} all-to-all(f32[16,512,128]{2,1,0:T(8,128)S(1)} %bitcast.35), channel_id=1, replica_groups=mesh['group'=8,'member_0'=2,'member_1'=4,'member_2'=2] {'member_0','memb..., dimensions={0} | all-to-all | bytes 8388608 | tf_op jit(solution)/shard_map/all_to_all | solution.py:36
  304.1 2.4 reduce_sum.18
  306.5 1.1 broadcast_in_dim.14
  307.6 4.0 all-to-all-start.1
  311.6 15.4 %all-to-all-done.1 = bf16[8,512,128]{2,1,0:T(8,128)(2,1)S(1)} async-done(((bf16[8,512,128]{2,1,0:T(8,128)(2,1)}), bf16[8,512,128]{2,1,0:T(8,128)(2,1)S(1)}, u32[]{:S(2)}, u32[]{:S(2)}) %all-to-all-start.1) | async-done | bytes 1048608 | tf_op jit(solution)/shard_map/all_to_all | solution.py:48
  327.1 0.5 copy.4
  327.6 4.4 fusion.26
  332.0 0.0 all-gather.13.cloned.1.call-start
  332.1 21.6 %all-gather.11.cloned.1.call-done = f32[2048,1024]{1,0:T(8,128)} async-done(((f32[1024,1024]{1,0:T(8,128)}), f32[2048,1024]{1,0:T(8,128)}) %all-gather.11.cloned.1.call-update) | async-done | bytes 8388624 | tf_op jit(solution)/shard_map/all_gather | solution.py:64
  353.7 6.8 %slice_add_fusion.4 = f32[1024,1024]{1,0:T(8,128)} fusion(f32[2048,1024]{1,0:T(8,128)} %all-gather.11.cloned.1.call-done), kind=kLoop, calls=%fused_computation.10 | loop fusion | flops 1048576 | bytes 12582912 | tf_op jit(solution)/shard_map/add | solution.py:81
  360.5 0.0 all-gather.9.cloned.1.call-start
  360.5 155.2 %all-gather.13.cloned.1.call-done = f32[4096,1024]{1,0:T(8,128)} async-done(((f32[1024,1024]{1,0:T(8,128)}), f32[4096,1024]{1,0:T(8,128)}) %all-gather.13.cloned.1.call-update) | async-done | bytes 16777232 | tf_op jit(solution)/shard_map/all_gather | solution.py:64
  515.7 10.3 %fusion.5 = f32[1,1024,1024]{2,1,0:T(8,128)} fusion(f32[4096,1024]{1,0:T(8,128)} %all-gather.13.cloned.1.call-done), kind=kLoop, calls=%fused_computation.7 | loop fusion | flops 3145728 | bytes 20971520 | tf_op jit(solution)/shard_map/add | solution.py:81
  526.0 0.7 multiply_reduce_fusion
  526.7 65.5 %psum.7 = f32[]{:T(128)} all-reduce(f32[]{:T(128)} %multiply_reduce_fusion), channel_id=1, replica_groups=mesh['group'=8,'member_0'=2,'member_1'=4,'member_2'=2] {'group','member_..., use_global_device_ids=true, to_apply=%region_3.4 | all-reduce | flops 1 | bytes 8 | tf_op jit(solution)/shard_map/psum | solution.py:92
  592.9 1.7 fusion.25
  594.6 39.9 %all-gather.9.cloned.1.call-done = f32[2,1024,1024]{2,1,0:T(8,128)} async-done(((f32[1,1024,1024]{2,1,0:T(8,128)}), f32[2,1024,1024]{2,1,0:T(8,128)}) %all-gather.9.cloned.1.call-update) | async-done | bytes 8388624 | tf_op jit(solution)/shard_map/all_gather | solution.py:64
  634.5 11.4 %fusion.3 = f32[512,1024]{1,0:T(8,128)S(1)} fusion(bf16[512,1024]{0,1:T(8,128)(2,1)S(1)} %bitcast.37, f32[2,1024,1024]{2,1,0:T(8,128)} %all-gather.9.cloned.1.call-done, f32[1,1024,1024]{2,1,0:T(8,128)} %fusion.5, f32[1024,1024]{1,0:T(8,128)} %slice_add_fusion.4, f32[4096,1024]{1,0:T(8,128)} %all-gather.13.cloned.1.call-done, ...), kind=kOutput, calls=%fused_computation.5 | convolution fusion | flops 6456082432 | bytes 36700168 | tf_op jit(solution)/shard_map/dot_general | solution.py:105
  646.0 4.4 subtract_convert_fusion
  (17 shorter events, 0.2 us)
Async XLA Ops:
  6.5 234.7 %copy-start = (bf16[8192,128]{1,0:T(8,128)(2,1)S(1)}, bf16[8192,128]{1,0:T(8,128)(2,1)}, u32[]{:S(2)}) copy-start(bf16[8192,128]{1,0:T(8,128)(2,1)} %param.5) | copy-start | bytes 6291460
  6.5 125.5 %reduce-scatter.2.cloned.1.call-start = ((), (), s32[]{:S(2)}) async-start(), calls=%async_computation.3 | async-start | bytes 9437184 | tf_op jit(solution)/shard_map/reduce_scatter | solution.py:25
  11.1 230.1 %all-gather.7.cloned.1.call-start = ((), (), s32[]{:S(2)}) async-start(), calls=%async_computation.4 | async-start | bytes 9437184 | tf_op jit(solution)/shard_map/all_gather | solution.py:26
  241.3 5.9 copy-start.2
  307.6 19.5 %all-to-all-start.1 = ((bf16[8,512,128]{2,1,0:T(8,128)(2,1)}), bf16[8,512,128]{2,1,0:T(8,128)(2,1)S(1)}, u32[]{:S(2)}, u32[]{:S(2)}) async-start(bf16[8,512,128]{2,1,0:T(8,128)(2,1)} %broadcast_in_dim.14), calls=%async_computation.2 | async-start | bytes 2097152 | tf_op jit(solution)/shard_map/all_to_all | solution.py:48
  311.6 42.1 %all-gather.11.cloned.1.call-start = ((), (), s32[]{:S(2)}) async-start(), calls=%async_computation.6 | async-start | bytes 12582912 | tf_op jit(solution)/shard_map/all_gather | solution.py:64
  332.0 183.6 %all-gather.13.cloned.1.call-start = ((), (), s32[]{:S(2)}) async-start(), calls=%async_computation.7 | async-start | bytes 20971520 | tf_op jit(solution)/shard_map/all_gather | solution.py:64
  360.5 274.1 %all-gather.9.cloned.1.call-start = ((), (), s32[]{:S(2)}) async-start(), calls=%async_computation.5 | async-start | bytes 12582912 | tf_op jit(solution)/shard_map/all_gather | solution.py:64
  634.5 11.4 %copy-start.3 = (f32[512,512]{1,0:T(8,128)S(1)}, f32[512,512]{1,0:T(8,128)}, u32[]{:S(2)}) copy-start(f32[512,512]{1,0:T(8,128)} %fusion.25) | copy-start | bytes 3145732
  634.5 15.8 %copy-start.1 = (bf16[8192,128]{1,0:T(8,128)(2,1)S(1)}, bf16[8192,128]{1,0:T(8,128)(2,1)}, u32[]{:S(2)}) copy-start(bf16[8192,128]{1,0:T(8,128)(2,1)} %param.5) | copy-start | bytes 6291460
Sparse Core Ops, SparseCore 0:
  11.3 120.6 reduce-scatter.1
  134.3 106.8 all-gather.6
  332.2 21.4 all-gather.10
  360.6 155.0 all-gather.12
  526.1 108.3 all-gather.8
where the time goes:
time: 656 us; the launch traced here: 657 us
  waiting for transfers between devices  462 us (70%)
  blocking collectives  120 us (18%)
  matrix products  30.2 us (5%)
  other arithmetic  23.9 us (4%)
  between operations  14.7 us (2%)
    all_gather x3, waiting for transfers between devices, prefix_by_axis(): pieces = lax.all_gather(total, axis)  217 us
    reduce_scatter x1, waiting for transfers between devices, broadcast_by_parts(): own = lax.psum_scatter(padded, axis, scatter_dimension=0, tiled=True)  121 us
    all_gather x1, waiting for transfers between devices, broadcast_by_parts(): lax.all_gather(own, axis, axis=0, tiled=True)[:len(lines)]  109 us
    psum x1, blocking collectives, shards(): square_total = lax.psum(jnp.sum(precond_wide * precond_wide), GROUP_MEMBER)  65.5 us
    all_to_all x1, blocking collectives, sum_at_owner(): tiles = lax.all_to_all(cut_along(value, dim, peers), axis, 0, 0, tiled=True)  54.6 us
    add x2, other arithmetic, add_blocks(): return earlier_sum + later_sum  17.1 us
    all_to_all x1, waiting for transfers between devices, sent_to_all(): return lax.all_to_all(copies, axis, split_axis=0, concat_axis=0, tiled=True)  15.4 us
  transfers between devices with their start and end apart: 6, of which 6 were waited for; matrix products, arithmetic and copies ran while one was open for 0% of the time, Pallas kernels for 0%

commit v1 on v0

v1 whole, which is shorter than its diff:
```python
import jax
import jax.numpy as jnp
from jax import lax
from jax.experimental import pallas as pl
from jax.experimental.pallas import tpu as pltpu
from jax.sharding import Mesh
from jax.sharding import PartitionSpec as P

GROUP = ("x", "yh")
CHIP = ("yl", "z")
MEMBER = ("yl", "z", "core")
GROUP_CHIP = GROUP + CHIP
bf16 = jnp.bfloat16
f32 = jnp.float32
params = pltpu.CompilerParams(vmem_limit_bytes=48 * 1024 * 1024)


def call(body, out, *args, scalars=0, scratch=()):
    vmem = pl.BlockSpec(memory_space=pltpu.VMEM)
    smem = pl.BlockSpec(memory_space=pltpu.SMEM)
    specs = [smem] * scalars + [vmem] * (len(args) - scalars)
    return pl.pallas_call(
        body,
        out_shape=out,
        in_specs=specs,
        out_specs=jax.tree.map(lambda _: vmem, out),
        scratch_shapes=scratch,
        compiler_params=params,
    )(*args)


def shape(dims, dtype=bf16):
    return jax.ShapeDtypeStruct(dims, dtype)


def contract(left, right, a, b):
    return lax.dot_general(left, right, (((a,), (b,)), ((), ())), preferred_element_type=f32)


def joined(ref):
    return jnp.concatenate([ref[b] for b in range(8)], axis=1)


def shift_x(value, step):
    return lax.ppermute(value, "x", [(i, (i + step) % 4) for i in range(4)])


def flip(value, axis):
    return lax.ppermute(value, axis, [(0, 1), (1, 0)])


def copies_to(value, axes):
    return lax.all_to_all(jnp.broadcast_to(value, (8, *value.shape)), axes, 0, 0, tiled=True)


def exchange(tiles, axes):
    return lax.all_to_all(tiles, axes, 0, 0, tiled=True)


def scatter_columns(panel, owner):
    rx = (lax.axis_index("x") - owner // 2) % 4
    ry = (lax.axis_index("yh") - owner % 2) % 2

    def block(i, j):
        g = ((owner // 2 + i) % 4) * 2 + (owner % 2 + j) % 2
        return lax.dynamic_slice_in_dim(panel, g * 1024, 1024, 1)

    to_right = shift_x(block(1, 1), 1)
    to_left = shift_x(block(3, 1), 3)
    across = flip(block(2, 1), "yh")
    far = jnp.where(ry == 0, block(2, 0), across)
    far_right = shift_x(far[:256], 1)
    far_left = shift_x(far[256:], 3)
    across2 = flip(jnp.where(rx == 0, block(0, 1), jnp.where(rx == 1, to_right, to_left)), "yh")
    relay = jnp.concatenate([far_right, far_left], axis=0)
    near_right = shift_x(jnp.where(rx == 0, block(1, 0), relay), 1)
    near_left = shift_x(jnp.where(rx == 0, block(3, 0), relay), 3)
    met = jnp.concatenate([near_right[:256], near_left[256:]], axis=0)
    result = jnp.where(rx == 1, near_right, jnp.where(rx == 3, near_left, met))
    result = jnp.where((ry == 1) & (rx != 2), across2, result)
    return jnp.where((ry == 0) & (rx == 0), block(0, 0), result)


def gradient_rows(grads, member, core):
    piece = lax.dynamic_index_in_dim(grads.reshape(8, 16, 64, 128), member, 1, keepdims=False)
    piece = exchange(piece, GROUP)
    mine = copies_to(piece, CHIP)
    other = flip(mine, "core")
    low = jnp.where(core == 0, mine, other)
    high = jnp.where(core == 0, other, mine)
    rows = jnp.stack([low, high], axis=1)
    return rows.transpose(0, 1, 3, 2, 4).reshape(1024, 1024)


def project_body(a_ref, g_ref, o_ref):
    a = a_ref[...]
    for j in range(4):
        value = jnp.dot(a, g_ref[:, 256 * j : 256 * j + 256], preferred_element_type=f32)
        o_ref[2 * j] = value[:, :128].astype(bf16)
        o_ref[2 * j + 1] = value[:, 128:].astype(bf16)


def spread_body(t_ref, o_ref):
    total = t_ref[0].astype(f32)
    for k in range(1, 8):
        total = total + t_ref[k].astype(f32)
    total = total.astype(bf16)
    for k in range(8):
        o_ref[k] = total


def total_body(t_ref, o_ref):
    total = t_ref[0].astype(f32)
    for k in range(1, 8):
        total = total + t_ref[k].astype(f32)
    o_ref[...] = total.astype(bf16)


def half_of(a_ref, half):
    return a_ref[:, pl.ds(pl.multiple_of(half * 512, 512), 512)]


def give_body(core_ref, a_ref, p_ref, o_ref):
    a = half_of(a_ref, 1 - core_ref[0])
    for j in range(4):
        p = jnp.concatenate([p_ref[2 * j], p_ref[2 * j + 1]], axis=1)
        value = contract(a, p, 0, 0)
        o_ref[2 * j] = value[:, :128].astype(bf16)
        o_ref[2 * j + 1] = value[:, 128:].astype(bf16)


def keep_body(core_ref, a_ref, p_ref, r_ref, o_ref):
    a = half_of(a_ref, core_ref[0])
    for j in range(4):
        p = jnp.concatenate([p_ref[2 * j], p_ref[2 * j + 1]], axis=1)
        value = contract(a, p, 0, 0)
        o_ref[2 * j] = (value[:, :128] + r_ref[2 * j].astype(f32)).astype(bf16)
        o_ref[2 * j + 1] = (value[:, 128:] + r_ref[2 * j + 1].astype(f32)).astype(bf16)


def outer_body(core_ref, q_ref, r_ref, a_ref, b_ref, o_ref):
    a = half_of(a_ref, core_ref[0])
    b = b_ref[...]
    squares = jnp.zeros((8, 128), f32)
    for j in range(4):
        q = jnp.concatenate([q_ref[2 * j], q_ref[2 * j + 1]], axis=1)
        r = jnp.concatenate([r_ref[2 * j], r_ref[2 * j + 1]], axis=1)
        value = (contract(q, a, 0, 0) + contract(r, b, 0, 0)).astype(bf16)
        o_ref[2 * j, :128] = value[:128]
        o_ref[2 * j + 1, :128] = value[128:]
        wide = q.astype(f32)
        squares = squares + jnp.sum((wide * wide).reshape(64, 8, 2, 128), axis=(0, 2))
        wide = r.astype(f32)
        squares = squares + jnp.sum((wide * wide).reshape(64, 8, 2, 128), axis=(0, 2))
    total = jnp.broadcast_to(jnp.sum(squares, axis=(0, 1), keepdims=True), (16, 512))
    top = total.astype(bf16)
    rest = total - top.astype(f32)
    middle = rest.astype(bf16)
    bottom = (rest - middle.astype(f32)).astype(bf16)
    row = lax.broadcasted_iota(jnp.int32, (16, 512), 0)
    tail = jnp.where(row == 0, top.astype(f32), jnp.where(row == 1, middle.astype(f32), bottom.astype(f32)))
    for j in range(8):
        o_ref[j, 128:] = tail.astype(bf16)


def suffix_body(t_ref, o_ref, s_ref):
    total = jnp.zeros((128, 512), f32)
    squares = jnp.zeros((1, 128), f32)
    for k in reversed(range(8)):
        o_ref[k] = total.astype(bf16)
        total = total + t_ref[k, :128].astype(f32)
        tail = t_ref[k, 128:, :128].astype(f32)
        squares = squares + (tail[0:1] + tail[1:2] + tail[2:3])
    s_ref[...] = jnp.broadcast_to(squares, (8, 128))


def near_body(core_ref, q_ref, r_ref, a_ref, b_ref, o_ref):
    core = core_ref[0]
    q = joined(q_ref)
    r = joined(r_ref)
    a = half_of(a_ref, core)
    b = b_ref[...]
    upper = lax.broadcasted_iota(jnp.int32, (512, 512), 0) <= lax.broadcasted_iota(jnp.int32, (512, 512), 1)
    o_ref[0] = jnp.dot(jnp.where(upper, contract(q, q, 1, 1), 0.0).astype(bf16), a, preferred_element_type=f32)
    o_ref[1] = jnp.dot(jnp.where(upper, contract(r, r, 1, 1), 0.0).astype(bf16), b, preferred_element_type=f32)

    @pl.when(core == 0)
    def _():
        o_ref[0] += jnp.dot(contract(q, r, 1, 1).astype(bf16), b, preferred_element_type=f32)

    @pl.when(core == 1)
    def _():
        o_ref[1] += jnp.dot(contract(r, q, 1, 1).astype(bf16), a, preferred_element_type=f32)


def update_body(core_ref, q_ref, r_ref, s_ref, n_ref, a_ref, b_ref, m_ref, o_ref, p_ref):
    a = half_of(a_ref, core_ref[0])
    b = b_ref[...]
    s = s_ref[...].reshape(1024, 512)
    rate = 1.0 / (1.0 + m_ref[0:1, 0:1] * (1.0 / 8388608.0))
    for ref, out, base, k in ((q_ref, o_ref, a, 0), (r_ref, p_ref, b, 1)):
        combined = n_ref[k] + jnp.dot(joined(ref), s, preferred_element_type=f32)
        out[...] = ((1.0 + rate) * base.astype(f32) - (rate * (1.0 / 1024.0)) * combined).astype(bf16)


def shards(factors, owner, grads):
    core = lax.axis_index("core")
    cores = core[None].astype(jnp.int32)
    member = lax.axis_index(MEMBER)
    own = scatter_columns(factors[0], owner[0])
    rows = gradient_rows(grads, member, core)
    tiles = shape((8, 512, 128))
    projected = call(project_body, tiles, own, rows)
    projected = exchange(projected, GROUP)
    projected = exchange(call(spread_body, tiles, projected), GROUP)
    given = flip(call(give_body, tiles, cores, own, projected, scalars=1), "core")
    kept = call(keep_body, tiles, cores, own, projected, given, scalars=1)
    other_own = flip(lax.dynamic_slice_in_dim(own, (1 - core) * 512, 512, 1), "core")
    piece = call(total_body, shape((512, 128)), exchange(kept, CHIP))
    swap = []
    for x in range(4):
        for yh in range(2):
            for yl in range(2):
                for z in range(4):
                    g, c = x * 2 + yh, yl * 4 + z
                    swap.append((g * 8 + c, c * 8 + g))
    piece = lax.ppermute(piece, GROUP_CHIP, swap)
    precond = copies_to(piece, GROUP)
    other = flip(precond, "core")
    products = call(outer_body, shape((8, 144, 512)), cores, precond, other, own, other_own, scalars=1)
    near = call(near_body, shape((2, 512, 512), f32), cores, precond, other, own, other_own, scalars=1)
    products = exchange(products, CHIP)
    later, squares = call(suffix_body, (shape((8, 128, 512)), shape((8, 128), f32)), products)
    later = exchange(later, CHIP)
    half = shape((512, 512))
    mine, theirs = call(
        update_body, (half, half), cores, precond, other, later, near, own, other_own, squares, scalars=1
    )
    theirs = flip(theirs, "core")
    left = jnp.where(core == 0, mine, theirs)
    right = jnp.where(core == 0, theirs, mine)
    return jnp.concatenate([left, right], axis=1)


def solution(mesh):
    split = Mesh(mesh.devices.reshape(4, 2, 2, 4, 2), GROUP + MEMBER)
    in_specs = (P(GROUP, MEMBER, None), P(), P(None, GROUP))
    out_specs = P(MEMBER, GROUP)
    return jax.shard_map(shards, mesh=split, in_specs=in_specs, out_specs=out_specs, check_vma=False)
```

time: 656 us -> 247 us (0.38)
  waiting for transfers between devices: 462 us -> 55.8 us
  starting transfers between devices: 4.13 us -> 43.9 us
  matrix products: 30.2 us -> 0 us
  blocking collectives: 120 us -> 102 us
  Pallas kernels: 0 us -> 16.3 us
  local copies, waits for them, and re-layouts: 1.64 us -> 16 us
  between operations: 14.7 us -> 1.13 us
  other arithmetic: 23.9 us -> 11.8 us
    all_gather x4 -> x0, waiting for transfers between devices: 326 us -> none  [the longest x3 217 us: prefix_by_axis(): pieces = lax.all_gather(total, axis)]
    reduce_scatter x1 -> x0, waiting for transfers between devices: 121 us -> none  [broadcast_by_parts(): own = lax.psum_scatter(padded, axis, scatter_dimension=0, tiled=True)]
    psum x1 -> x0, blocking collectives: 65.5 us -> none  [shards(): square_total = lax.psum(jnp.sum(precond_wide * precond_wide), GROUP_MEMBER)]
    all_to_all x1 -> x5, blocking collectives: 54.6 us -> 102 us  [the longest x4 71 us: exchange(): return lax.all_to_all(tiles, axes, 0, 0, tiled=True)]
    dot_general x6 -> x0, matrix products: 30.2 us -> none  [the longest x1 11.4 us: shards(): jnp.dot(left_rows.astype(jnp.float32), tail_total, precision=highest)]
    ppermute x0 -> x14, starting transfers between devices: none -> 29.5 us  [the longest x7 21.2 us: flip(): return lax.ppermute(value, axis, [(0, 1), (1, 0)])]
    ppermute x0 -> x14, waiting for transfers between devices: none -> 25 us  [the longest x6 18.3 us: shift_x(): return lax.ppermute(value, 'x', [(i, (i + step) % 4) for i in range(4)])]
    add x3 -> x0, other arithmetic: 17.1 us -> none  [the longest x2 17.1 us: add_blocks(): return earlier_sum + later_sum]
  transfers between devices with their start and end apart: 6 -> 17, of which waited for: 6 -> 9; matrix products, arithmetic and copies ran while one was open for 0% -> 7% of each run, Pallas kernels for 0% -> 2%
where the time goes in v1:
time: 247 us; the launch traced here: 246 us
  blocking collectives  102 us (41%)
  waiting for transfers between devices  55.8 us (23%)
  starting transfers between devices  43.9 us (18%)
  Pallas kernels  16.3 us (7%)
  local copies, waits for them, and re-layouts  16 us (6%)
  other arithmetic  11.8 us (5%)
    all_to_all x4, blocking collectives, exchange(): return lax.all_to_all(tiles, axes, 0, 0, tiled=True)  71 us
    all_to_all x1, blocking collectives, copies_to(): lax.all_to_all(jnp.broadcast_to(value, (8, *value.shape)), axes, 0, 0, ti...  30.6 us
    all_to_all x2, waiting for transfers between devices, exchange(): return lax.all_to_all(tiles, axes, 0, 0, tiled=True)  22.7 us
    ppermute x7, starting transfers between devices, flip(): return lax.ppermute(value, axis, [(0, 1), (1, 0)])  21.2 us
    ppermute x6, waiting for transfers between devices, shift_x(): return lax.ppermute(value, 'x', [(i, (i + step) % 4) for i in range(4)])  18.3 us
    pallas_call x9, Pallas kernels, call(): pl.pallas_call(body, out_shape=out, in_specs=specs, out_specs=jax.tree.ma...  16.3 us
    all_to_all x2, starting transfers between devices, exchange(): return lax.all_to_all(tiles, axes, 0, 0, tiled=True)  8.28 us
    all_to_all x1, waiting for transfers between devices, copies_to(): lax.all_to_all(jnp.broadcast_to(value, (8, *value.shape)), axes, 0, 0, ti...  8.05 us
  transfers between devices with their start and end apart: 17, of which 9 were waited for; matrix products, arithmetic and copies ran while one was open for 7% of the time, Pallas kernels for 2%

profile of v1, /device:TPU:1, one launch (start us, length us, event | category | flops | bytes accessed | tf_op | source)
XLA Modules:
  0.0 246.5 jit_solution(13506427788931695758)
XLA Ops:
  0.9 3.6 %dynamic-slice_bitcast_fusion = (bf16[512,1024]{1,0:T(8,128)(2,1)}, bf16[512,1024]{1,0:T(8,128)(2,1)}, bf16[512,1024]{1,0:T(8,128)(2,1)}) fusion(bf16[1,512,8192]{2,1,0:T(8,128)(2,1)} %param.3, s32[]{:T(128)S(6)} %select_n.216, s32[]{:T(128)S(6)} %select_n.209, s32[]{:T(128)S(6)} %select_n.207), kind=kLoop, calls=%fused_computation.13 | loop fusion | bytes 6291468 | tf_op jit(solution)/shard_map/dynamic_slice | solution.py:66
  4.5 3.7 %collective-permute-start.3 = (bf16[512,1024]{1,0:T(8,128)(2,1)}, bf16[512,1024]{1,0:T(8,128)(2,1)}, u32[]{:S(2)}, u32[]{:S(2)}) collective-permute-start(bf16[512,1024]{1,0:T(8,128)(2,1)} %get-tuple-element.16), channel_id=1, source_target_pairs={{0,16},{16,0},{1,17},{17,1},{2,18},{18,2},{3,19},{19,3},{4,20},{20... | collective-permute-start | bytes 3145736 | tf_op jit(solution)/shard_map/ppermute | solution.py:49
  8.9 4.0 %all-to-all-start = ((bf16[8,64,128]{2,1,0:T(8,128)(2,1)}), bf16[8,64,128]{2,1,0:T(8,128)(2,1)S(1)}, u32[]{:S(2)}, u32[]{:S(2)}) async-start(bf16[8,64,128]{2,1,0:T(8,128)(2,1)} %dynamic-slice_bitcast_fusion.3), calls=%async_computation | async-start | bytes 262144 | tf_op jit(solution)/shard_map/all_to_all | solution.py:57
  15.7 16.9 %all-to-all-done = bf16[8,64,128]{2,1,0:T(8,128)(2,1)S(1)} async-done(((bf16[8,64,128]{2,1,0:T(8,128)(2,1)}), bf16[8,64,128]{2,1,0:T(8,128)(2,1)S(1)}, u32[]{:S(2)}, u32[]{:S(2)}) %all-to-all-start) | async-done | bytes 131104 | tf_op jit(solution)/shard_map/all_to_all | solution.py:57
  33.8 6.1 %all-to-all-start.1 = ((bf16[8,8,64,128]{3,1,2,0:T(8,128)(2,1)}), bf16[8,8,64,128]{3,1,2,0:T(8,128)(2,1)S(1)}, u32[]{:S(2)}, u32[]{:S(2)}) async-start(bf16[8,8,64,128]{3,1,2,0:T(8,128)(2,1)} %broadcast_in_dim.10), calls=%async_computation.1 | async-start | bytes 2097152 | tf_op jit(solution)/shard_map/all_to_all | solution.py:53
  45.2 8.1 %all-to-all-done.1 = bf16[8,8,64,128]{3,1,2,0:T(8,128)(2,1)S(1)} async-done(((bf16[8,8,64,128]{3,1,2,0:T(8,128)(2,1)}), bf16[8,8,64,128]{3,1,2,0:T(8,128)(2,1)S(1)}, u32[]{:S(2)}, u32[]{:S(2)}) %all-to-all-start.1) | async-done | bytes 1048608 | tf_op jit(solution)/shard_map/all_to_all | solution.py:53
  58.0 5.0 %bitcast_select_fusion = (bf16[512,1024]{1,0:T(8,128)(2,1)}, bf16[512,1024]{1,0:T(8,128)(2,1)}, bf16[512,1024]{1,0:T(8,128)(2,1)}) fusion(bf16[512,1024]{1,0:T(8,128)(2,1)S(1)} %constant_dynamic-update-slice_fusion, bf16[1,512,8192]{2,1,0:T(8,128)(2,1)} %param.3, s32[]{:T(128)S(6)} %select_n.220, pred[]{:T(512)S(6)} %eq.56, s32[]{:T(128)S(6)} %select_n.212, ...), kind=kLoop, calls=%fused_computation.7 | loop fusion | flops 2097152 | bytes 9437198 | tf_op jit(solution)/shard_map/jit(_where)/select_n | solution.py:77
  65.3 2.6 %collective-permute-start.2 = (bf16[512,1024]{1,0:T(8,128)(2,1)}, bf16[512,1024]{1,0:T(8,128)(2,1)}, u32[]{:S(2)}, u32[]{:S(2)}) collective-permute-start(bf16[512,1024]{1,0:T(8,128)(2,1)} %get-tuple-element.15), channel_id=1, source_target_pairs={{0,16},{16,0},{1,17},{17,1},{2,18},{18,2},{3,19},{19,3},{4,20},{20... | collective-permute-start | bytes 3145736 | tf_op jit(solution)/shard_map/ppermute | solution.py:49
  70.1 16.0 %collective-permute-done.7 = bf16[512,1024]{1,0:T(8,128)(2,1)} collective-permute-done((bf16[512,1024]{1,0:T(8,128)(2,1)}, bf16[512,1024]{1,0:T(8,128)(2,1)}, u32[]{:S(2)}, u32[]{:S(2)}) %collective-permute-start.7) | collective-permute-done | bytes 1048608 | tf_op jit(solution)/shard_map/ppermute | solution.py:45
  90.3 2.4 fusion.2.a_ref
  94.0 17.6 %all_to_all.40.t_ref = bf16[8,512,128]{2,1,0:T(8,128)(2,1)S(1)} all-to-all(bf16[8,512,128]{2,1,0:T(8,128)(2,1)S(1)} %shard_map.37), channel_id=1, replica_groups=mesh['x'=4,'yh'=2,'yl'=2,'z'=4,'core'=2] {'x','yh'}, dimensions={0} | all-to-all | bytes 2097152 | tf_op jit(solution)/shard_map/all_to_all | solution.py:57
  111.8 14.8 %all_to_all.41.p_ref = bf16[8,512,128]{2,1,0:T(8,128)(2,1)S(1)} all-to-all(bf16[8,512,128]{2,1,0:T(8,128)(2,1)S(1)} %shard_map.38), channel_id=1, replica_groups=mesh['x'=4,'yh'=2,'yl'=2,'z'=4,'core'=2] {'x','yh'}, dimensions={0} | all-to-all | bytes 2097152 | tf_op jit(solution)/shard_map/all_to_all | solution.py:57
  127.3 6.6 %collective-permute-start.9 = (bf16[8,512,128]{2,1,0:T(8,128)(2,1)S(1)}, bf16[8,512,128]{2,1,0:T(8,128)(2,1)S(1)}, u32[]{:S(2)}, u32[]{:S(2)}) collective-permute-start(bf16[8,512,128]{2,1,0:T(8,128)(2,1)S(1)} %shard_map.39), channel_id=1, source_target_pairs={{0,1},{1,0},{2,3},{3,2},{4,5},{5,4},{6,7},{7,6},{8,9},{9,8},{10,11... | collective-permute-start | bytes 3145736 | tf_op jit(solution)/shard_map/ppermute | solution.py:49
  136.9 16.9 %all_to_all.42.t_ref = bf16[8,512,128]{2,1,0:T(8,128)(2,1)S(1)} all-to-all(bf16[8,512,128]{2,1,0:T(8,128)(2,1)S(1)} %shard_map.40), channel_id=1, replica_groups=mesh['x'=4,'yh'=2,'yl'=2,'z'=4,'core'=2] {'yl','z'}, dimensions={0} | all-to-all | bytes 2097152 | tf_op jit(solution)/shard_map/all_to_all | solution.py:57
  154.8 30.6 %all_to_all.43.q_ref = bf16[8,512,128]{2,1,0:T(8,128)(2,1)} all-to-all(bf16[8,512,128]{2,1,0:T(8,128)(2,1)S(1)} %broadcast_in_dim.11), channel_id=1, replica_groups=mesh['x'=4,'yh'=2,'yl'=2,'z'=4,'core'=2] {'x','yh'}, dimensions={0} | all-to-all | bytes 2097152 | tf_op jit(solution)/shard_map/all_to_all | solution.py:53
  185.4 2.6 %collective-permute-start.11 = (bf16[8,512,128]{2,1,0:T(8,128)(2,1)}, bf16[8,512,128]{2,1,0:T(8,128)(2,1)}, u32[]{:S(2)}, u32[]{:S(2)}) collective-permute-start(bf16[8,512,128]{2,1,0:T(8,128)(2,1)} %all_to_all.43.q_ref), channel_id=1, source_target_pairs={{0,1},{1,0},{2,3},{3,2},{4,5},{5,4},{6,7},{7,6},{8,9},{9,8},{10,11... | collective-permute-start | bytes 3145736 | tf_op jit(solution)/shard_map/ppermute | solution.py:49
  188.1 2.9 %collective-permute-done.12.b_ref = bf16[512,512]{1,0:T(8,128)(2,1)S(1)} collective-permute-done((bf16[512,512]{1,0:T(8,128)(2,1)S(1)}, bf16[512,512]{1,0:T(8,128)(2,1)S(1)}, u32[]{:S(2)}, u32[]{:S(2)}) %collective-permute-start.12) | collective-permute-done | bytes 524320 | tf_op jit(solution)/shard_map/ppermute | solution.py:49
  191.1 4.9 %shard_map.42 = bf16[8,144,512]{2,1,0:T(8,128)(2,1)S(1)} custom-call(s32[1]{0:T(128)} %bitcast.core_ref, bf16[8,512,128]{2,1,0:T(8,128)(2,1)} %all_to_all.43.q_ref, bf16[8,512,128]{2,1,0:T(8,128)(2,1)} %collective-permute-done.11.r_ref, bf16[512,1024]{1,0:T(8,128)(2,1)S(1)} %fusion.2.a_ref, bf16[512,512]{1,0:T(8,128)(2,1)S(1)} %collective-permute-done.12.b_ref), custom_call_target="tpu_custom_call" | custom-call | tf_op jit(solution)/shard_map/pallas_call | solution.py:22
  195.9 21.7 %all_to_all.44.t_ref = bf16[8,144,512]{2,1,0:T(8,128)(2,1)S(1)} all-to-all(bf16[8,144,512]{2,1,0:T(8,128)(2,1)S(1)} %shard_map.42), channel_id=1, replica_groups=mesh['x'=4,'yh'=2,'yl'=2,'z'=4,'core'=2] {'yl','z'}, dimensions={0} | all-to-all | bytes 2359296 | tf_op jit(solution)/shard_map/all_to_all | solution.py:57
  218.8 4.3 %all-to-all-start.7 = ((bf16[8,128,512]{2,1,0:T(8,128)(2,1)}), bf16[8,128,512]{2,1,0:T(8,128)(2,1)}, u32[]{:S(2)}, u32[]{:S(2)}) async-start(bf16[8,128,512]{2,1,0:T(8,128)(2,1)} %copy-done.5), calls=%async_computation.7 | async-start | bytes 2097152 | tf_op jit(solution)/shard_map/all_to_all | solution.py:57
  224.1 4.4 %shard_map.44.n_ref = f32[2,512,512]{2,1,0:T(8,128)S(1)} custom-call(s32[1]{0:T(128)} %bitcast.core_ref, bf16[8,512,128]{2,1,0:T(8,128)(2,1)} %all_to_all.43.q_ref, bf16[8,512,128]{2,1,0:T(8,128)(2,1)} %collective-permute-done.11.r_ref, bf16[512,1024]{1,0:T(8,128)(2,1)S(1)} %fusion.2.a_ref, bf16[512,512]{1,0:T(8,128)(2,1)S(1)} %copy-done.3), custom_call_target="tpu_custom_call" | custom-call | tf_op jit(solution)/shard_map/pallas_call | solution.py:22
  229.9 5.8 %all-to-all-done.7.s_ref = bf16[8,128,512]{2,1,0:T(8,128)(2,1)} async-done(((bf16[8,128,512]{2,1,0:T(8,128)(2,1)}), bf16[8,128,512]{2,1,0:T(8,128)(2,1)}, u32[]{:S(2)}, u32[]{:S(2)}) %all-to-all-start.7) | async-done | bytes 1048608 | tf_op jit(solution)/shard_map/all_to_all | solution.py:57
  236.7 3.8 %shard_map.45 = (bf16[512,512]{1,0:T(8,128)(2,1)S(1)}, bf16[512,512]{1,0:T(8,128)(2,1)S(1)}) custom-call(s32[1]{0:T(128)} %bitcast.core_ref, bf16[8,512,128]{2,1,0:T(8,128)(2,1)} %all_to_all.43.q_ref, bf16[8,512,128]{2,1,0:T(8,128)(2,1)} %collective-permute-done.11.r_ref, bf16[8,128,512]{2,1,0:T(8,128)(2,1)} %all-to-all-done.7.s_ref, ...), custom_call_target="tpu_custom_call" | custom-call | tf_op jit(solution)/shard_map/pallas_call | solution.py:22
  240.5 3.2 %collective-permute-start.13 = (bf16[512,512]{1,0:T(8,128)(2,1)S(1)}, bf16[512,512]{1,0:T(8,128)(2,1)S(1)}, u32[]{:S(2)}, u32[]{:S(2)}) collective-permute-start(bf16[512,512]{1,0:T(8,128)(2,1)S(1)} %get-tuple-element.12), channel_id=1, source_target_pairs={{0,1},{1,0},{2,3},{3,2},{4,5},{5,4},{6,7},{7,6},{8,9},{9,8},{10,11... | collective-permute-start | bytes 1572872 | tf_op jit(solution)/shard_map/ppermute | solution.py:49
  (55 shorter events, 36.8 us)
Async XLA Ops:
  0.0 8.3 %copy-start = (bf16[8192,128]{1,0:T(8,128)(2,1)S(1)}, bf16[8192,128]{1,0:T(8,128)(2,1)}, u32[]{:S(2)}) copy-start(bf16[8192,128]{1,0:T(8,128)(2,1)} %param.5) | copy-start | bytes 6291460
  4.5 35.3 %collective-permute-start.3 = (bf16[512,1024]{1,0:T(8,128)(2,1)}, bf16[512,1024]{1,0:T(8,128)(2,1)}, u32[]{:S(2)}, u32[]{:S(2)}) collective-permute-start(bf16[512,1024]{1,0:T(8,128)(2,1)} %get-tuple-element.16), channel_id=1, source_target_pairs={{0,16},{16,0},{1,17},{17,1},{2,18},{18,2},{3,19},{19,3},{4,20},{20... | collective-permute-start | bytes 3145736 | tf_op jit(solution)/shard_map/ppermute | solution.py:49
  8.9 23.6 %all-to-all-start = ((bf16[8,64,128]{2,1,0:T(8,128)(2,1)}), bf16[8,64,128]{2,1,0:T(8,128)(2,1)S(1)}, u32[]{:S(2)}, u32[]{:S(2)}) async-start(bf16[8,64,128]{2,1,0:T(8,128)(2,1)} %dynamic-slice_bitcast_fusion.3), calls=%async_computation | async-start | bytes 262144 | tf_op jit(solution)/shard_map/all_to_all | solution.py:57
  13.0 45.0 %collective-permute-start = (bf16[512,1024]{1,0:T(8,128)(2,1)}, bf16[512,1024]{1,0:T(8,128)(2,1)}, u32[]{:S(2)}, u32[]{:S(2)}) collective-permute-start(bf16[512,1024]{1,0:T(8,128)(2,1)} %get-tuple-element.18), channel_id=1, source_target_pairs={{0,32},{32,64},{64,96},{96,0},{1,33},{33,65},{65,97},{97,1},{2,34}... | collective-permute-start | bytes 3145736 | tf_op jit(solution)/shard_map/ppermute | solution.py:45
  14.4 43.6 %collective-permute-start.1 = (bf16[512,1024]{1,0:T(8,128)(2,1)}, bf16[512,1024]{1,0:T(8,128)(2,1)}, u32[]{:S(2)}, u32[]{:S(2)}) collective-permute-start(bf16[512,1024]{1,0:T(8,128)(2,1)} %get-tuple-element.17), channel_id=1, source_target_pairs={{0,96},{32,0},{64,32},{96,64},{1,97},{33,1},{65,33},{97,65},{2,98}... | collective-permute-start | bytes 3145736 | tf_op jit(solution)/shard_map/ppermute | solution.py:45
  33.8 19.5 %all-to-all-start.1 = ((bf16[8,8,64,128]{3,1,2,0:T(8,128)(2,1)}), bf16[8,8,64,128]{3,1,2,0:T(8,128)(2,1)S(1)}, u32[]{:S(2)}, u32[]{:S(2)}) async-start(bf16[8,8,64,128]{3,1,2,0:T(8,128)(2,1)} %broadcast_in_dim.10), calls=%async_computation.1 | async-start | bytes 2097152 | tf_op jit(solution)/shard_map/all_to_all | solution.py:53
  42.6 13.2 %collective-permute-start.4 = (bf16[256,1024]{1,0:T(8,128)(2,1)}, bf16[256,1024]{1,0:T(8,128)(2,1)}, u32[]{:S(2)}, u32[]{:S(2)}) collective-permute-start(bf16[256,1024]{1,0:T(8,128)(2,1)} %get-tuple-element.24), channel_id=1, source_target_pairs={{0,32},{32,64},{64,96},{96,0},{1,33},{33,65},{65,97},{97,1},{2,34}... | collective-permute-start | bytes 1572872 | tf_op jit(solution)/shard_map/ppermute | solution.py:45
  43.8 13.1 %collective-permute-start.5 = (bf16[256,1024]{1,0:T(8,128)(2,1)}, bf16[256,1024]{1,0:T(8,128)(2,1)}, u32[]{:S(2)}, u32[]{:S(2)}) collective-permute-start(bf16[256,1024]{1,0:T(8,128)(2,1)} %get-tuple-element.23), channel_id=1, source_target_pairs={{0,96},{32,0},{64,32},{96,64},{1,97},{33,1},{65,33},{97,65},{2,98}... | collective-permute-start | bytes 1572872 | tf_op jit(solution)/shard_map/ppermute | solution.py:45
  53.3 14.6 %collective-permute-start.8 = (bf16[8,8,64,128]{3,1,2,0:T(8,128)(2,1)S(1)}, bf16[8,8,64,128]{3,1,2,0:T(8,128)(2,1)}, u32[]{:S(2)}, u32[]{:S(2)}) collective-permute-start(bf16[8,8,64,128]{3,1,2,0:T(8,128)(2,1)S(1)} %all-to-all-done.1), channel_id=1, source_target_pairs={{0,1},{1,0},{2,3},{3,2},{4,5},{5,4},{6,7},{7,6},{8,9},{9,8},{10,11... | collective-permute-start | bytes 3145736 | tf_op jit(solution)/shard_map/ppermute | solution.py:49
  63.0 23.2 %collective-permute-start.7 = (bf16[512,1024]{1,0:T(8,128)(2,1)}, bf16[512,1024]{1,0:T(8,128)(2,1)}, u32[]{:S(2)}, u32[]{:S(2)}) collective-permute-start(bf16[512,1024]{1,0:T(8,128)(2,1)} %get-tuple-element.13), channel_id=1, source_target_pairs={{0,96},{32,0},{64,32},{96,64},{1,97},{33,1},{65,33},{97,65},{2,98}... | collective-permute-start | bytes 3145736 | tf_op jit(solution)/shard_map/ppermute | solution.py:45
  65.3 24.0 %collective-permute-start.6 = (bf16[512,1024]{1,0:T(8,128)(2,1)}, bf16[512,1024]{1,0:T(8,128)(2,1)}, u32[]{:S(2)}, u32[]{:S(2)}) collective-permute-start(bf16[512,1024]{1,0:T(8,128)(2,1)} %get-tuple-element.14), channel_id=1, source_target_pairs={{0,32},{32,64},{64,96},{96,0},{1,33},{33,65},{65,97},{97,1},{2,34}... | collective-permute-start | bytes 3145736 | tf_op jit(solution)/shard_map/ppermute | solution.py:45
  65.3 25.1 %collective-permute-start.2 = (bf16[512,1024]{1,0:T(8,128)(2,1)}, bf16[512,1024]{1,0:T(8,128)(2,1)}, u32[]{:S(2)}, u32[]{:S(2)}) collective-permute-start(bf16[512,1024]{1,0:T(8,128)(2,1)} %get-tuple-element.15), channel_id=1, source_target_pairs={{0,16},{16,0},{1,17},{17,1},{2,18},{18,2},{3,19},{19,3},{4,20},{20... | collective-permute-start | bytes 3145736 | tf_op jit(solution)/shard_map/ppermute | solution.py:49
  127.3 8.9 %collective-permute-start.9 = (bf16[8,512,128]{2,1,0:T(8,128)(2,1)S(1)}, bf16[8,512,128]{2,1,0:T(8,128)(2,1)S(1)}, u32[]{:S(2)}, u32[]{:S(2)}) collective-permute-start(bf16[8,512,128]{2,1,0:T(8,128)(2,1)S(1)} %shard_map.39), channel_id=1, source_target_pairs={{0,1},{1,0},{2,3},{3,2},{4,5},{5,4},{6,7},{7,6},{8,9},{9,8},{10,11... | collective-permute-start | bytes 3145736 | tf_op jit(solution)/shard_map/ppermute | solution.py:49
  154.0 0.7 collective-permute-start.10
  185.4 5.6 %collective-permute-start.11 = (bf16[8,512,128]{2,1,0:T(8,128)(2,1)}, bf16[8,512,128]{2,1,0:T(8,128)(2,1)}, u32[]{:S(2)}, u32[]{:S(2)}) collective-permute-start(bf16[8,512,128]{2,1,0:T(8,128)(2,1)} %all_to_all.43.q_ref), channel_id=1, source_target_pairs={{0,1},{1,0},{2,3},{3,2},{4,5},{5,4},{6,7},{7,6},{8,9},{9,8},{10,11... | collective-permute-start | bytes 3145736 | tf_op jit(solution)/shard_map/ppermute | solution.py:49
  188.0 3.0 %collective-permute-start.12 = (bf16[512,512]{1,0:T(8,128)(2,1)S(1)}, bf16[512,512]{1,0:T(8,128)(2,1)S(1)}, u32[]{:S(2)}, u32[]{:S(2)}) collective-permute-start(bf16[512,512]{1,0:T(8,128)(2,1)S(1)} %constant_dynamic-slice_fusion), channel_id=1, source_target_pairs={{0,1},{1,0},{2,3},{3,2},{4,5},{5,4},{6,7},{7,6},{8,9},{9,8},{10,11... | collective-permute-start | bytes 1572872 | tf_op jit(solution)/shard_map/ppermute | solution.py:49
  191.0 4.9 %copy-start.2 = (bf16[512,512]{1,0:T(8,128)(2,1)}, bf16[512,512]{1,0:T(8,128)(2,1)S(1)}, u32[]{:S(2)}) copy-start(bf16[512,512]{1,0:T(8,128)(2,1)S(1)} %collective-permute-done.12.b_ref) | copy-start | bytes 1572868
  217.8 1.0 copy-start.5
  218.8 16.9 %all-to-all-start.7 = ((bf16[8,128,512]{2,1,0:T(8,128)(2,1)}), bf16[8,128,512]{2,1,0:T(8,128)(2,1)}, u32[]{:S(2)}, u32[]{:S(2)}) async-start(bf16[8,128,512]{2,1,0:T(8,128)(2,1)} %copy-done.5), calls=%async_computation.7 | async-start | bytes 2097152 | tf_op jit(solution)/shard_map/all_to_all | solution.py:57
  223.1 1.0 copy-start.3
  228.5 1.4 copy-start.1
  235.6 1.0 copy-start.4
  240.5 4.8 %collective-permute-start.13 = (bf16[512,512]{1,0:T(8,128)(2,1)S(1)}, bf16[512,512]{1,0:T(8,128)(2,1)S(1)}, u32[]{:S(2)}, u32[]{:S(2)}) collective-permute-start(bf16[512,512]{1,0:T(8,128)(2,1)S(1)} %get-tuple-element.12), channel_id=1, source_target_pairs={{0,1},{1,0},{2,3},{3,2},{4,5},{5,4},{6,7},{7,6},{8,9},{9,8},{10,11... | collective-permute-start | bytes 1572872 | tf_op jit(solution)/shard_map/ppermute | solution.py:49

commit v2 on v1

--- a/solution.py
+++ b/solution.py
@@ -57,45 +57,139 @@
     return lax.all_to_all(tiles, axes, 0, 0, tiled=True)
 
 
+def copy_blocks(panel_ref, sems, *pairs):
+    copies = []
+    for column, out_ref in pairs:
+        start = pl.multiple_of(column * 1024, 1024)
+        for top in (0, 128, 256, 384):
+            source = panel_ref.at[pl.ds(top, 128), pl.ds(start, 1024)]
+            copies.append(pltpu.make_async_copy(source, out_ref.at[pl.ds(top, 128)], sems.at[len(copies)]))
+    for copy in copies:
+        copy.start()
+    for copy in copies:
+        copy.wait()
+
+
+FAR, DOWN, RIGHT, LEFT, HERE, CORE = 2, 3, 4, 5, 6, 7
+
+
+def second_body(plan_ref, panel_ref, right_ref, left_ref, across_ref, upper_ref, lower_ref, cross_ref, far_ref, sems):
+    column, row = plan_ref[0], plan_ref[1]
+
+    @pl.when((column == 0) & (row == 0))
+    def _():
+        copy_blocks(panel_ref, sems, (plan_ref[FAR], far_ref), (plan_ref[DOWN], cross_ref))
+        upper_ref[...] = far_ref[:256]
+        lower_ref[...] = far_ref[256:]
+
+    @pl.when((column != 0) | (row != 0))
+    def _():
+        upper_ref[...] = across_ref[:256]
+        lower_ref[...] = across_ref[256:]
+
+    @pl.when(column == 1)
+    def _():
+        cross_ref[...] = right_ref[...]
+
+    @pl.when((column != 1) & ((column != 0) | (row != 0)))
+    def _():
+        cross_ref[...] = left_ref[...]
+
+
+def third_body(plan_ref, panel_ref, right_ref, left_ref, to_right_ref, to_left_ref, sems):
+    @pl.when(plan_ref[0] == 0)
+    def _():
+        copy_blocks(panel_ref, sems, (plan_ref[RIGHT], to_right_ref), (plan_ref[LEFT], to_left_ref))
+
+    @pl.when(plan_ref[0] > 0)
+    def _():
+        for ref in (to_right_ref, to_left_ref):
+            ref[:256] = right_ref[...]
+            ref[256:] = left_ref[...]
+
+
+def with_panel(body, out, plan, panel, *received, scratch=()):
+    vmem = pl.BlockSpec(memory_space=pltpu.VMEM)
+    return pl.pallas_call(
+        body,
+        out_shape=out,
+        in_specs=[pl.BlockSpec(memory_space=pltpu.SMEM), pl.BlockSpec(memory_space=pl.ANY)] + [vmem] * len(received),
+        out_specs=jax.tree.map(lambda _: vmem, out),
+        scratch_shapes=(*scratch, pltpu.SemaphoreType.DMA((8,))),
+        compiler_params=params,
+    )(plan, panel, *received)
+
+
 def scatter_columns(panel, owner):
     rx = (lax.axis_index("x") - owner // 2) % 4
     ry = (lax.axis_index("yh") - owner % 2) % 2
 
+    def column(i, j):
+        return ((owner // 2 + i) % 4) * 2 + (owner % 2 + j) % 2
+
     def block(i, j):
-        g = ((owner // 2 + i) % 4) * 2 + (owner % 2 + j) % 2
-        return lax.dynamic_slice_in_dim(panel, g * 1024, 1024, 1)
-
+        return lax.dynamic_slice_in_dim(panel, column(i, j) * 1024, 1024, 1)
+
+    places = [column(2, 0), column(0, 1), column(1, 0), column(3, 0), column(0, 0)]
+    plan = jnp.stack([rx, ry, *places, lax.axis_index("core")]).astype(jnp.int32)
+    full, half = shape((512, 1024)), shape((256, 1024))
     to_right = shift_x(block(1, 1), 1)
     to_left = shift_x(block(3, 1), 3)
     across = flip(block(2, 1), "yh")
-    far = jnp.where(ry == 0, block(2, 0), across)
-    far_right = shift_x(far[:256], 1)
-    far_left = shift_x(far[256:], 3)
-    across2 = flip(jnp.where(rx == 0, block(0, 1), jnp.where(rx == 1, to_right, to_left)), "yh")
-    relay = jnp.concatenate([far_right, far_left], axis=0)
-    near_right = shift_x(jnp.where(rx == 0, block(1, 0), relay), 1)
-    near_left = shift_x(jnp.where(rx == 0, block(3, 0), relay), 3)
-    met = jnp.concatenate([near_right[:256], near_left[256:]], axis=0)
-    result = jnp.where(rx == 1, near_right, jnp.where(rx == 3, near_left, met))
-    result = jnp.where((ry == 1) & (rx != 2), across2, result)
-    return jnp.where((ry == 0) & (rx == 0), block(0, 0), result)
-
-
-def gradient_rows(grads, member, core):
-    piece = lax.dynamic_index_in_dim(grads.reshape(8, 16, 64, 128), member, 1, keepdims=False)
-    piece = exchange(piece, GROUP)
-    mine = copies_to(piece, CHIP)
-    other = flip(mine, "core")
-    low = jnp.where(core == 0, mine, other)
-    high = jnp.where(core == 0, other, mine)
-    rows = jnp.stack([low, high], axis=1)
-    return rows.transpose(0, 1, 3, 2, 4).reshape(1024, 1024)
-
-
-def project_body(a_ref, g_ref, o_ref):
-    a = a_ref[...]
+    upper, lower, crossing = with_panel(
+        second_body, (half, half, full), plan, panel, to_right, to_left, across,
+        scratch=(pltpu.VMEM((512, 1024), bf16),),
+    )
+    across = flip(crossing, "yh")
+    far_right = shift_x(upper, 1)
+    far_left = shift_x(lower, 3)
+    near_right, near_left = with_panel(third_body, (full, full), plan, panel, far_right, far_left)
+    return plan, (shift_x(near_right, 1), shift_x(near_left, 3), across)
+
+
+def half_body(core_ref, g_ref, o_ref):
+    pltpu.sync_copy(g_ref.at[:, core_ref[0]], o_ref)
+
+
+def gradient_half(grads, cores):
+    return pl.pallas_call(
+        half_body,
+        out_shape=shape((8, 512, 128)),
+        in_specs=[pl.BlockSpec(memory_space=pltpu.SMEM), pl.BlockSpec(memory_space=pl.ANY)],
+        out_specs=pl.BlockSpec(memory_space=pltpu.VMEM),
+    )(cores, grads.reshape(8, 2, 512, 128))
+
+
+def project_body(plan_ref, panel_ref, g_ref, h_ref, right_ref, left_ref, across_ref, a_ref, o_ref, sems):
+    column, row = plan_ref[0], plan_ref[1]
+    straight = row == 0
+
+    @pl.when((column == 0) & straight)
+    def _():
+        copy_blocks(panel_ref, sems, (plan_ref[HERE], a_ref))
+
+    @pl.when((column == 1) & straight)
+    def _():
+        a_ref[...] = right_ref[...]
+
+    @pl.when((column == 3) & straight)
+    def _():
+        a_ref[...] = left_ref[...]
+
+    @pl.when(column == 2)
+    def _():
+        a_ref[:256] = right_ref[:256]
+        a_ref[256:] = left_ref[256:]
+
+    @pl.when((column != 2) & (row == 1))
+    def _():
+        a_ref[...] = across_ref[...]
+
+    mine, other = half_of(a_ref, plan_ref[CORE]), half_of(a_ref, 1 - plan_ref[CORE])
     for j in range(4):
-        value = jnp.dot(a, g_ref[:, 256 * j : 256 * j + 256], preferred_element_type=f32)
+        g = jnp.concatenate([g_ref[2 * j], g_ref[2 * j + 1]], axis=1)
+        h = jnp.concatenate([h_ref[2 * j], h_ref[2 * j + 1]], axis=1)
+        value = jnp.dot(mine, g, preferred_element_type=f32) + jnp.dot(other, h, preferred_element_type=f32)
         o_ref[2 * j] = value[:, :128].astype(bf16)
         o_ref[2 * j + 1] = value[:, 128:].astype(bf16)
 
@@ -180,17 +274,23 @@
     r = joined(r_ref)
     a = half_of(a_ref, core)
     b = b_ref[...]
+
+    def times(gram, rows):
+        top = gram.astype(bf16)
+        rest = (gram - top.astype(f32)).astype(bf16)
+        return jnp.dot(top, rows, preferred_element_type=f32) + jnp.dot(rest, rows, preferred_element_type=f32)
+
     upper = lax.broadcasted_iota(jnp.int32, (512, 512), 0) <= lax.broadcasted_iota(jnp.int32, (512, 512), 1)
-    o_ref[0] = jnp.dot(jnp.where(upper, contract(q, q, 1, 1), 0.0).astype(bf16), a, preferred_element_type=f32)
-    o_ref[1] = jnp.dot(jnp.where(upper, contract(r, r, 1, 1), 0.0).astype(bf16), b, preferred_element_type=f32)
+    o_ref[0] = times(jnp.where(upper, contract(q, q, 1, 1), 0.0), a)
+    o_ref[1] = times(jnp.where(upper, contract(r, r, 1, 1), 0.0), b)
 
     @pl.when(core == 0)
     def _():
-        o_ref[0] += jnp.dot(contract(q, r, 1, 1).astype(bf16), b, preferred_element_type=f32)
+        o_ref[0] += times(contract(q, r, 1, 1), b)
 
     @pl.when(core == 1)
     def _():
-        o_ref[1] += jnp.dot(contract(r, q, 1, 1).astype(bf16), a, preferred_element_type=f32)
+        o_ref[1] += times(contract(r, q, 1, 1), a)
 
 
 def update_body(core_ref, q_ref, r_ref, s_ref, n_ref, a_ref, b_ref, m_ref, o_ref, p_ref):
@@ -206,11 +306,10 @@
 def shards(factors, owner, grads):
     core = lax.axis_index("core")
     cores = core[None].astype(jnp.int32)
-    member = lax.axis_index(MEMBER)
-    own = scatter_columns(factors[0], owner[0])
-    rows = gradient_rows(grads, member, core)
+    mine = exchange(gradient_half(grads, cores), GROUP)
+    plan, received = scatter_columns(factors[0], owner[0])
     tiles = shape((8, 512, 128))
-    projected = call(project_body, tiles, own, rows)
+    own, projected = with_panel(project_body, (shape((512, 1024)), tiles), plan, factors[0], mine, flip(mine, "core"), *received)
     projected = exchange(projected, GROUP)
     projected = exchange(call(spread_body, tiles, projected), GROUP)
     given = flip(call(give_body, tiles, cores, own, projected, scalars=1), "core")

time: 247 us -> 238 us (0.964)
  other arithmetic: 11.8 us -> 2.21 us
  Pallas kernels: 16.3 us -> 21.1 us
  local copies, waits for them, and re-layouts: 16 us -> 11.9 us
    ppermute x7, waiting for transfers between devices: 6.74 us -> 35.7 us  [flip(): return lax.ppermute(value, axis, [(0, 1), (1, 0)])]
    all_to_all x2, waiting for transfers between devices: 22.7 us -> 6.54 us  [exchange(): return lax.all_to_all(tiles, axes, 0, 0, tiled=True)]
    select_n x3 -> x0, other arithmetic: 9.02 us -> none  [the longest x1 4.98 us: scatter_columns(): near_left = shift_x(jnp.where(rx == 0, block(3, 0), relay), 3)]
    pallas_call x0 -> x4, Pallas kernels: none -> 8.37 us  [the longest x3 6.18 us: with_panel(): pl.pallas_call(body, out_shape=out, in_specs=[pl.BlockSpec(memory_space=p...]
    all_to_all x1 -> x0, waiting for transfers between devices: 8.05 us -> none  [copies_to(): lax.all_to_all(jnp.broadcast_to(value, (8, *value.shape)), axes, 0, 0, ti...]
    all_to_all x1 -> x0, starting transfers between devices: 6.07 us -> none  [copies_to(): lax.all_to_all(jnp.broadcast_to(value, (8, *value.shape)), axes, 0, 0, ti...]
    ppermute x6, waiting for transfers between devices: 18.3 us -> 13.7 us  [shift_x(): return lax.ppermute(value, 'x', [(i, (i + step) % 4) for i in range(4)])]
    ppermute x7, starting transfers between devices: 21.2 us -> 25.5 us  [flip(): return lax.ppermute(value, axis, [(0, 1), (1, 0)])]
  transfers between devices with their start and end apart: 17 -> 16, of which waited for: 9 -> 7; matrix products, arithmetic and copies ran while one was open for 7% -> 0% of each run, Pallas kernels for 2% -> 4%
where the time goes in v2:
time: 238 us; the launch traced here: 237 us
  blocking collectives  102 us (43%)
  waiting for transfers between devices  55.9 us (23%)
  starting transfers between devices  42.7 us (18%)
  Pallas kernels  21.1 us (9%)
  local copies, waits for them, and re-layouts  11.9 us (5%)
    all_to_all x4, blocking collectives, exchange(): return lax.all_to_all(tiles, axes, 0, 0, tiled=True)  71.2 us
    ppermute x7, waiting for transfers between devices, flip(): return lax.ppermute(value, axis, [(0, 1), (1, 0)])  35.7 us
    all_to_all x1, blocking collectives, copies_to(): lax.all_to_all(jnp.broadcast_to(value, (8, *value.shape)), axes, 0, 0, ti...  30.7 us
    ppermute x7, starting transfers between devices, flip(): return lax.ppermute(value, axis, [(0, 1), (1, 0)])  25.5 us
    ppermute x6, waiting for transfers between devices, shift_x(): return lax.ppermute(value, 'x', [(i, (i + step) % 4) for i in range(4)])  13.7 us
    pallas_call x8, Pallas kernels, call(): pl.pallas_call(body, out_shape=out, in_specs=specs, out_specs=jax.tree.ma...  12.7 us
    ppermute x6, starting transfers between devices, shift_x(): return lax.ppermute(value, 'x', [(i, (i + step) % 4) for i in range(4)])  8.73 us
    unnamed x18, local copies, waits for them, and re-layouts  8.08 us
  transfers between devices with their start and end apart: 16, of which 7 were waited for; matrix products, arithmetic and copies ran while one was open for 0% of the time, Pallas kernels for 4%

profile of v2, /device:TPU:1, one launch (start us, length us, event | category | flops | bytes accessed | tf_op | source)
XLA Modules:
  0.0 236.8 jit_solution(9533428271913202095)
XLA Ops:
  0.8 3.6 %dynamic-slice_bitcast_fusion = (bf16[512,1024]{1,0:T(8,128)(2,1)}, bf16[512,1024]{1,0:T(8,128)(2,1)}, bf16[512,1024]{1,0:T(8,128)(2,1)}) fusion(bf16[1,512,8192]{2,1,0:T(8,128)(2,1)} %param.3, s32[]{:T(128)S(6)} %select_n.124, s32[]{:T(128)S(6)} %select_n.122, s32[]{:T(128)S(6)} %select_n.123), kind=kLoop, calls=%fused_computation.1 | loop fusion | bytes 6291468 | tf_op jit(solution)/shard_map/dynamic_slice | solution.py:131
  7.7 3.1 %collective-permute-start.3 = (bf16[512,1024]{1,0:T(8,128)(2,1)}, bf16[512,1024]{1,0:T(8,128)(2,1)}, u32[]{:S(2)}, u32[]{:S(2)}) collective-permute-start(bf16[512,1024]{1,0:T(8,128)(2,1)} %get-tuple-element.27), channel_id=1, source_target_pairs={{0,16},{16,0},{1,17},{17,1},{2,18},{18,2},{3,19},{19,3},{4,20},{20... | collective-permute-start | bytes 3145736 | tf_op jit(solution)/shard_map/ppermute | solution.py:49
  13.0 3.6 %all-to-all-start = ((bf16[8,512,128]{2,1,0:T(8,128)(2,1)}), bf16[8,512,128]{2,1,0:T(8,128)(2,1)S(1)}, u32[]{:S(2)}, u32[]{:S(2)}) async-start(bf16[8,512,128]{2,1,0:T(8,128)(2,1)} %shard_map.37), calls=%async_computation | async-start | bytes 2097152 | tf_op jit(solution)/shard_map/all_to_all | solution.py:57
  16.7 13.7 %collective-permute-done.1.right_ref = bf16[512,1024]{1,0:T(8,128)(2,1)S(1)} collective-permute-done((bf16[512,1024]{1,0:T(8,128)(2,1)}, bf16[512,1024]{1,0:T(8,128)(2,1)S(1)}, u32[]{:S(2)}, u32[]{:S(2)}) %collective-permute-start.1) | collective-permute-done | bytes 1048608 | tf_op jit(solution)/shard_map/ppermute | solution.py:45
  30.4 8.5 %collective-permute-done.3.across_ref = bf16[512,1024]{1,0:T(8,128)(2,1)} collective-permute-done((bf16[512,1024]{1,0:T(8,128)(2,1)}, bf16[512,1024]{1,0:T(8,128)(2,1)}, u32[]{:S(2)}, u32[]{:S(2)}) %collective-permute-start.3) | collective-permute-done | bytes 1048608 | tf_op jit(solution)/shard_map/ppermute | solution.py:49
  42.4 2.7 %collective-permute-start.5 = (bf16[256,1024]{1,0:T(8,128)(2,1)}, bf16[256,1024]{1,0:T(8,128)(2,1)S(1)}, u32[]{:S(2)}, u32[]{:S(2)}) collective-permute-start(bf16[256,1024]{1,0:T(8,128)(2,1)} %get-tuple-element.17), channel_id=1, source_target_pairs={{0,96},{32,0},{64,32},{96,64},{1,97},{33,1},{65,33},{97,65},{2,98}... | collective-permute-start | bytes 1572872 | tf_op jit(solution)/shard_map/ppermute | solution.py:45
  45.0 5.9 %collective-permute-start = (bf16[8,512,128]{2,1,0:T(8,128)(2,1)S(1)}, bf16[8,512,128]{2,1,0:T(8,128)(2,1)S(1)}, u32[]{:S(2)}, u32[]{:S(2)}) collective-permute-start(bf16[8,512,128]{2,1,0:T(8,128)(2,1)S(1)} %all-to-all-done.g_ref), channel_id=1, source_target_pairs={{0,1},{1,0},{2,3},{3,2},{4,5},{5,4},{6,7},{7,6},{8,9},{9,8},{10,11... | collective-permute-start | bytes 3145736 | tf_op jit(solution)/shard_map/ppermute | solution.py:49
  51.0 3.7 %collective-permute-start.8 = (bf16[512,1024]{1,0:T(8,128)(2,1)}, bf16[512,1024]{1,0:T(8,128)(2,1)S(1)}, u32[]{:S(2)}, u32[]{:S(2)}) collective-permute-start(bf16[512,1024]{1,0:T(8,128)(2,1)} %copy-done.6), channel_id=1, source_target_pairs={{0,16},{16,0},{1,17},{17,1},{2,18},{18,2},{3,19},{19,3},{4,20},{20... | collective-permute-start | bytes 3145736 | tf_op jit(solution)/shard_map/ppermute | solution.py:49
  58.2 20.2 %collective-permute-done.8.across_ref = bf16[512,1024]{1,0:T(8,128)(2,1)S(1)} collective-permute-done((bf16[512,1024]{1,0:T(8,128)(2,1)}, bf16[512,1024]{1,0:T(8,128)(2,1)S(1)}, u32[]{:S(2)}, u32[]{:S(2)}) %collective-permute-start.8) | collective-permute-done | bytes 1048608 | tf_op jit(solution)/shard_map/ppermute | solution.py:49
  80.3 3.0 %shard_map.40 = (bf16[512,1024]{1,0:T(8,128)(2,1)S(1)}, bf16[8,512,128]{2,1,0:T(8,128)(2,1)S(1)}) custom-call(s32[8]{0:T(128)S(1)} %stack.32.plan_ref, bf16[512,8192]{1,0:T(8,128)(2,1)} %bitcast.23, bf16[8,512,128]{2,1,0:T(8,128)(2,1)S(1)} %all-to-all-done.g_ref, bf16[8,512,128]{2,1,0:T(8,128)(2,1)S(1)} %collective-permute-done.h_ref, ...), custom_call_target="tpu_custom_call" | custom-call | tf_op jit(solution)/shard_map/pallas_call | solution.py:113
  83.3 16.5 %all_to_all.35.t_ref = bf16[8,512,128]{2,1,0:T(8,128)(2,1)S(1)} all-to-all(bf16[8,512,128]{2,1,0:T(8,128)(2,1)S(1)} %get-tuple-element.22), channel_id=1, replica_groups=mesh['x'=4,'yh'=2,'yl'=2,'z'=4,'core'=2] {'x','yh'}, dimensions={0} | all-to-all | bytes 2097152 | tf_op jit(solution)/shard_map/all_to_all | solution.py:57
  100.0 14.8 %all_to_all.36.p_ref = bf16[8,512,128]{2,1,0:T(8,128)(2,1)S(1)} all-to-all(bf16[8,512,128]{2,1,0:T(8,128)(2,1)S(1)} %shard_map.41), channel_id=1, replica_groups=mesh['x'=4,'yh'=2,'yl'=2,'z'=4,'core'=2] {'x','yh'}, dimensions={0} | all-to-all | bytes 2097152 | tf_op jit(solution)/shard_map/all_to_all | solution.py:57
  115.6 7.0 %collective-permute-start.9 = (bf16[8,512,128]{2,1,0:T(8,128)(2,1)S(1)}, bf16[8,512,128]{2,1,0:T(8,128)(2,1)S(1)}, u32[]{:S(2)}, u32[]{:S(2)}) collective-permute-start(bf16[8,512,128]{2,1,0:T(8,128)(2,1)S(1)} %shard_map.42), channel_id=1, source_target_pairs={{0,1},{1,0},{2,3},{3,2},{4,5},{5,4},{6,7},{7,6},{8,9},{9,8},{10,11... | collective-permute-start | bytes 3145736 | tf_op jit(solution)/shard_map/ppermute | solution.py:49
  125.6 19.4 %all_to_all.37.t_ref = bf16[8,512,128]{2,1,0:T(8,128)(2,1)S(1)} all-to-all(bf16[8,512,128]{2,1,0:T(8,128)(2,1)S(1)} %shard_map.43), channel_id=1, replica_groups=mesh['x'=4,'yh'=2,'yl'=2,'z'=4,'core'=2] {'yl','z'}, dimensions={0} | all-to-all | bytes 2097152 | tf_op jit(solution)/shard_map/all_to_all | solution.py:57
  145.9 30.7 %all_to_all.38.q_ref = bf16[8,512,128]{2,1,0:T(8,128)(2,1)S(1)} all-to-all(bf16[8,512,128]{2,1,0:T(8,128)(2,1)S(1)} %broadcast_in_dim.7), channel_id=1, replica_groups=mesh['x'=4,'yh'=2,'yl'=2,'z'=4,'core'=2] {'x','yh'}, dimensions={0} | all-to-all | bytes 2097152 | tf_op jit(solution)/shard_map/all_to_all | solution.py:53
  176.6 2.6 %collective-permute-start.11 = (bf16[8,512,128]{2,1,0:T(8,128)(2,1)S(1)}, bf16[8,512,128]{2,1,0:T(8,128)(2,1)S(1)}, u32[]{:S(2)}, u32[]{:S(2)}) collective-permute-start(bf16[8,512,128]{2,1,0:T(8,128)(2,1)S(1)} %all_to_all.38.q_ref), channel_id=1, source_target_pairs={{0,1},{1,0},{2,3},{3,2},{4,5},{5,4},{6,7},{7,6},{8,9},{9,8},{10,11... | collective-permute-start | bytes 3145736 | tf_op jit(solution)/shard_map/ppermute | solution.py:49
  179.3 2.9 %collective-permute-done.12.b_ref = bf16[512,512]{1,0:T(8,128)(2,1)S(1)} collective-permute-done((bf16[512,512]{1,0:T(8,128)(2,1)S(1)}, bf16[512,512]{1,0:T(8,128)(2,1)S(1)}, u32[]{:S(2)}, u32[]{:S(2)}) %collective-permute-start.12) | collective-permute-done | bytes 524320 | tf_op jit(solution)/shard_map/ppermute | solution.py:49
  182.2 3.1 %shard_map.45 = bf16[8,144,512]{2,1,0:T(8,128)(2,1)S(1)} custom-call(s32[1]{0:T(128)} %bitcast.core_ref, bf16[8,512,128]{2,1,0:T(8,128)(2,1)S(1)} %all_to_all.38.q_ref, bf16[8,512,128]{2,1,0:T(8,128)(2,1)S(1)} %collective-permute-done.11.r_ref, bf16[512,1024]{1,0:T(8,128)(2,1)S(1)} %get-tuple-element.21.a_ref, bf16[512,512]{1,0:T(8,128)(2,1)S(1)} %collective-permute-done.12.b_ref), custom_call_target="tpu_custom_call" | custom-call | tf_op jit(solution)/shard_map/pallas_call | solution.py:22
  185.4 20.5 %all_to_all.39.t_ref = bf16[8,144,512]{2,1,0:T(8,128)(2,1)S(1)} all-to-all(bf16[8,144,512]{2,1,0:T(8,128)(2,1)S(1)} %shard_map.45), channel_id=1, replica_groups=mesh['x'=4,'yh'=2,'yl'=2,'z'=4,'core'=2] {'yl','z'}, dimensions={0} | all-to-all | bytes 2359296 | tf_op jit(solution)/shard_map/all_to_all | solution.py:57
  207.0 4.2 %all-to-all-start.6 = ((bf16[8,128,512]{2,1,0:T(8,128)(2,1)}), bf16[8,128,512]{2,1,0:T(8,128)(2,1)}, u32[]{:S(2)}, u32[]{:S(2)}) async-start(bf16[8,128,512]{2,1,0:T(8,128)(2,1)} %copy-done.4), calls=%async_computation.6 | async-start | bytes 2097152 | tf_op jit(solution)/shard_map/all_to_all | solution.py:57
  212.3 3.7 %shard_map.47.n_ref = f32[2,512,512]{2,1,0:T(8,128)S(1)} custom-call(s32[1]{0:T(128)} %bitcast.core_ref, bf16[8,512,128]{2,1,0:T(8,128)(2,1)S(1)} %all_to_all.38.q_ref, bf16[8,512,128]{2,1,0:T(8,128)(2,1)S(1)} %collective-permute-done.11.r_ref, bf16[512,1024]{1,0:T(8,128)(2,1)S(1)} %get-tuple-element.21.a_ref, bf16[512,512]{1,0:T(8,128)(2,1)S(1)} %copy-done.2), custom_call_target="tpu_custom_call" | custom-call | tf_op jit(solution)/shard_map/pallas_call | solution.py:22
  217.4 6.5 %all-to-all-done.6.s_ref = bf16[8,128,512]{2,1,0:T(8,128)(2,1)} async-done(((bf16[8,128,512]{2,1,0:T(8,128)(2,1)}), bf16[8,128,512]{2,1,0:T(8,128)(2,1)}, u32[]{:S(2)}, u32[]{:S(2)}) %all-to-all-start.6) | async-done | bytes 1048608 | tf_op jit(solution)/shard_map/all_to_all | solution.py:57
  224.9 4.0 %shard_map.48 = (bf16[512,512]{1,0:T(8,128)(2,1)S(1)}, bf16[512,512]{1,0:T(8,128)(2,1)}) custom-call(s32[1]{0:T(128)} %bitcast.core_ref, bf16[8,512,128]{2,1,0:T(8,128)(2,1)S(1)} %all_to_all.38.q_ref, bf16[8,512,128]{2,1,0:T(8,128)(2,1)S(1)} %collective-permute-done.11.r_ref, bf16[8,128,512]{2,1,0:T(8,128)(2,1)} %all-to-all-done.6.s_ref, ...), custom_call_target="tpu_custom_call" | custom-call | tf_op jit(solution)/shard_map/pallas_call | solution.py:22
  229.7 3.1 %collective-permute-start.13 = (bf16[512,512]{1,0:T(8,128)(2,1)}, bf16[512,512]{1,0:T(8,128)(2,1)S(1)}, u32[]{:S(2)}, u32[]{:S(2)}) collective-permute-start(bf16[512,512]{1,0:T(8,128)(2,1)} %get-tuple-element.26), channel_id=1, source_target_pairs={{0,1},{1,0},{2,3},{3,2},{4,5},{5,4},{6,7},{7,6},{8,9},{9,8},{10,11... | collective-permute-start | bytes 1572872 | tf_op jit(solution)/shard_map/ppermute | solution.py:49
  (49 shorter events, 28.7 us)
Async XLA Ops:
  4.4 26.1 %collective-permute-start.1 = (bf16[512,1024]{1,0:T(8,128)(2,1)}, bf16[512,1024]{1,0:T(8,128)(2,1)S(1)}, u32[]{:S(2)}, u32[]{:S(2)}) collective-permute-start(bf16[512,1024]{1,0:T(8,128)(2,1)} %get-tuple-element.28), channel_id=1, source_target_pairs={{0,32},{32,64},{64,96},{96,0},{1,33},{33,65},{65,97},{97,1},{2,34}... | collective-permute-start | bytes 3145736 | tf_op jit(solution)/shard_map/ppermute | solution.py:45
  6.4 24.0 %collective-permute-start.2 = (bf16[512,1024]{1,0:T(8,128)(2,1)}, bf16[512,1024]{1,0:T(8,128)(2,1)S(1)}, u32[]{:S(2)}, u32[]{:S(2)}) collective-permute-start(bf16[512,1024]{1,0:T(8,128)(2,1)} %get-tuple-element.29), channel_id=1, source_target_pairs={{0,96},{32,0},{64,32},{96,64},{1,97},{33,1},{65,33},{97,65},{2,98}... | collective-permute-start | bytes 3145736 | tf_op jit(solution)/shard_map/ppermute | solution.py:45
  7.7 31.3 %collective-permute-start.3 = (bf16[512,1024]{1,0:T(8,128)(2,1)}, bf16[512,1024]{1,0:T(8,128)(2,1)}, u32[]{:S(2)}, u32[]{:S(2)}) collective-permute-start(bf16[512,1024]{1,0:T(8,128)(2,1)} %get-tuple-element.27), channel_id=1, source_target_pairs={{0,16},{16,0},{1,17},{17,1},{2,18},{18,2},{3,19},{19,3},{4,20},{20... | collective-permute-start | bytes 3145736 | tf_op jit(solution)/shard_map/ppermute | solution.py:49
  13.0 32.1 %all-to-all-start = ((bf16[8,512,128]{2,1,0:T(8,128)(2,1)}), bf16[8,512,128]{2,1,0:T(8,128)(2,1)S(1)}, u32[]{:S(2)}, u32[]{:S(2)}) async-start(bf16[8,512,128]{2,1,0:T(8,128)(2,1)} %shard_map.37), calls=%async_computation | async-start | bytes 2097152 | tf_op jit(solution)/shard_map/all_to_all | solution.py:57
  41.4 1.0 copy-start.6
  42.4 12.3 %collective-permute-start.4 = (bf16[256,1024]{1,0:T(8,128)(2,1)}, bf16[256,1024]{1,0:T(8,128)(2,1)S(1)}, u32[]{:S(2)}, u32[]{:S(2)}) collective-permute-start(bf16[256,1024]{1,0:T(8,128)(2,1)} %get-tuple-element.16), channel_id=1, source_target_pairs={{0,32},{32,64},{64,96},{96,0},{1,33},{33,65},{65,97},{97,1},{2,34}... | collective-permute-start | bytes 1572872 | tf_op jit(solution)/shard_map/ppermute | solution.py:45
  42.4 12.3 %collective-permute-start.5 = (bf16[256,1024]{1,0:T(8,128)(2,1)}, bf16[256,1024]{1,0:T(8,128)(2,1)S(1)}, u32[]{:S(2)}, u32[]{:S(2)}) collective-permute-start(bf16[256,1024]{1,0:T(8,128)(2,1)} %get-tuple-element.17), channel_id=1, source_target_pairs={{0,96},{32,0},{64,32},{96,64},{1,97},{33,1},{65,33},{97,65},{2,98}... | collective-permute-start | bytes 1572872 | tf_op jit(solution)/shard_map/ppermute | solution.py:45
  45.0 13.2 %collective-permute-start = (bf16[8,512,128]{2,1,0:T(8,128)(2,1)S(1)}, bf16[8,512,128]{2,1,0:T(8,128)(2,1)S(1)}, u32[]{:S(2)}, u32[]{:S(2)}) collective-permute-start(bf16[8,512,128]{2,1,0:T(8,128)(2,1)S(1)} %all-to-all-done.g_ref), channel_id=1, source_target_pairs={{0,1},{1,0},{2,3},{3,2},{4,5},{5,4},{6,7},{7,6},{8,9},{9,8},{10,11... | collective-permute-start | bytes 3145736 | tf_op jit(solution)/shard_map/ppermute | solution.py:49
  51.0 27.4 %collective-permute-start.8 = (bf16[512,1024]{1,0:T(8,128)(2,1)}, bf16[512,1024]{1,0:T(8,128)(2,1)S(1)}, u32[]{:S(2)}, u32[]{:S(2)}) collective-permute-start(bf16[512,1024]{1,0:T(8,128)(2,1)} %copy-done.6), channel_id=1, source_target_pairs={{0,16},{16,0},{1,17},{17,1},{2,18},{18,2},{3,19},{19,3},{4,20},{20... | collective-permute-start | bytes 3145736 | tf_op jit(solution)/shard_map/ppermute | solution.py:49
  55.4 23.0 %collective-permute-start.6 = (bf16[512,1024]{1,0:T(8,128)(2,1)S(1)}, bf16[512,1024]{1,0:T(8,128)(2,1)S(1)}, u32[]{:S(2)}, u32[]{:S(2)}) collective-permute-start(bf16[512,1024]{1,0:T(8,128)(2,1)S(1)} %get-tuple-element.18), channel_id=1, source_target_pairs={{0,32},{32,64},{64,96},{96,0},{1,33},{33,65},{65,97},{97,1},{2,34}... | collective-permute-start | bytes 3145736 | tf_op jit(solution)/shard_map/ppermute | solution.py:45
  57.1 21.3 %collective-permute-start.7 = (bf16[512,1024]{1,0:T(8,128)(2,1)S(1)}, bf16[512,1024]{1,0:T(8,128)(2,1)S(1)}, u32[]{:S(2)}, u32[]{:S(2)}) collective-permute-start(bf16[512,1024]{1,0:T(8,128)(2,1)S(1)} %get-tuple-element.19), channel_id=1, source_target_pairs={{0,96},{32,0},{64,32},{96,64},{1,97},{33,1},{65,33},{97,65},{2,98}... | collective-permute-start | bytes 3145736 | tf_op jit(solution)/shard_map/ppermute | solution.py:45
  78.4 1.0 copy-start.7
  79.4 1.0 copy-start.8
  115.6 9.3 %collective-permute-start.9 = (bf16[8,512,128]{2,1,0:T(8,128)(2,1)S(1)}, bf16[8,512,128]{2,1,0:T(8,128)(2,1)S(1)}, u32[]{:S(2)}, u32[]{:S(2)}) collective-permute-start(bf16[8,512,128]{2,1,0:T(8,128)(2,1)S(1)} %shard_map.42), channel_id=1, source_target_pairs={{0,1},{1,0},{2,3},{3,2},{4,5},{5,4},{6,7},{7,6},{8,9},{9,8},{10,11... | collective-permute-start | bytes 3145736 | tf_op jit(solution)/shard_map/ppermute | solution.py:49
  145.1 0.7 collective-permute-start.10
  176.6 5.6 %collective-permute-start.11 = (bf16[8,512,128]{2,1,0:T(8,128)(2,1)S(1)}, bf16[8,512,128]{2,1,0:T(8,128)(2,1)S(1)}, u32[]{:S(2)}, u32[]{:S(2)}) collective-permute-start(bf16[8,512,128]{2,1,0:T(8,128)(2,1)S(1)} %all_to_all.38.q_ref), channel_id=1, source_target_pairs={{0,1},{1,0},{2,3},{3,2},{4,5},{5,4},{6,7},{7,6},{8,9},{9,8},{10,11... | collective-permute-start | bytes 3145736 | tf_op jit(solution)/shard_map/ppermute | solution.py:49
  179.2 3.0 %collective-permute-start.12 = (bf16[512,512]{1,0:T(8,128)(2,1)S(1)}, bf16[512,512]{1,0:T(8,128)(2,1)S(1)}, u32[]{:S(2)}, u32[]{:S(2)}) collective-permute-start(bf16[512,512]{1,0:T(8,128)(2,1)S(1)} %constant_dynamic-slice_fusion), channel_id=1, source_target_pairs={{0,1},{1,0},{2,3},{3,2},{4,5},{5,4},{6,7},{7,6},{8,9},{9,8},{10,11... | collective-permute-start | bytes 1572872 | tf_op jit(solution)/shard_map/ppermute | solution.py:49
  182.2 3.2 %copy-start.1 = (bf16[512,512]{1,0:T(8,128)(2,1)}, bf16[512,512]{1,0:T(8,128)(2,1)S(1)}, u32[]{:S(2)}) copy-start(bf16[512,512]{1,0:T(8,128)(2,1)S(1)} %collective-permute-done.12.b_ref) | copy-start | bytes 1572868
  206.1 1.0 copy-start.4
  207.0 16.9 %all-to-all-start.6 = ((bf16[8,128,512]{2,1,0:T(8,128)(2,1)}), bf16[8,128,512]{2,1,0:T(8,128)(2,1)}, u32[]{:S(2)}, u32[]{:S(2)}) async-start(bf16[8,128,512]{2,1,0:T(8,128)(2,1)} %copy-done.4), calls=%async_computation.6 | async-start | bytes 2097152 | tf_op jit(solution)/shard_map/all_to_all | solution.py:57
  211.3 1.0 copy-start.2
  216.0 1.4 copy-start
  223.9 1.0 copy-start.3
  229.7 4.9 %collective-permute-start.13 = (bf16[512,512]{1,0:T(8,128)(2,1)}, bf16[512,512]{1,0:T(8,128)(2,1)S(1)}, u32[]{:S(2)}, u32[]{:S(2)}) collective-permute-start(bf16[512,512]{1,0:T(8,128)(2,1)} %get-tuple-element.26), channel_id=1, source_target_pairs={{0,1},{1,0},{2,3},{3,2},{4,5},{5,4},{6,7},{7,6},{8,9},{9,8},{10,11... | collective-permute-start | bytes 1572872 | tf_op jit(solution)/shard_map/ppermute | solution.py:49
  (1 other events, 0.8 us)

commit v3 on v2

--- a/solution.py
+++ b/solution.py
@@ -61,7 +61,7 @@
     copies = []
     for column, out_ref in pairs:
         start = pl.multiple_of(column * 1024, 1024)
-        for top in (0, 128, 256, 384):
+        for top in range(0, out_ref.shape[0], 128):
             source = panel_ref.at[pl.ds(top, 128), pl.ds(start, 1024)]
             copies.append(pltpu.make_async_copy(source, out_ref.at[pl.ds(top, 128)], sems.at[len(copies)]))
     for copy in copies:
@@ -70,31 +70,35 @@
         copy.wait()
 
 
-FAR, DOWN, RIGHT, LEFT, HERE, CORE = 2, 3, 4, 5, 6, 7
-
-
-def second_body(plan_ref, panel_ref, right_ref, left_ref, across_ref, upper_ref, lower_ref, cross_ref, far_ref, sems):
-    column, row = plan_ref[0], plan_ref[1]
-
-    @pl.when((column == 0) & (row == 0))
-    def _():
-        copy_blocks(panel_ref, sems, (plan_ref[FAR], far_ref), (plan_ref[DOWN], cross_ref))
+FAR, DOWN, RIGHT, LEFT, HERE, QUARTER = 2, 3, 4, 5, 6, 7
+
+
+def cross_body(plan_ref, panel_ref, right_ref, left_ref, cross_ref, sems):
+    @pl.when(plan_ref[0] == 0)
+    def _():
+        copy_blocks(panel_ref, sems, (plan_ref[DOWN], cross_ref))
+
+    @pl.when(plan_ref[0] == 1)
+    def _():
+        cross_ref[...] = right_ref[...]
+
+    @pl.when(plan_ref[0] > 1)
+    def _():
+        cross_ref[...] = left_ref[...]
+
+
+def far_body(plan_ref, panel_ref, across_ref, upper_ref, lower_ref, far_ref, sems):
+    @pl.when(plan_ref[1] == 0)
+    def _():
+        copy_blocks(panel_ref, sems, (plan_ref[FAR], far_ref))
         upper_ref[...] = far_ref[:256]
         lower_ref[...] = far_ref[256:]
 
-    @pl.when((column != 0) | (row != 0))
+    @pl.when(plan_ref[1] == 1)
     def _():
         upper_ref[...] = across_ref[:256]
         lower_ref[...] = across_ref[256:]
 
-    @pl.when(column == 1)
-    def _():
-        cross_ref[...] = right_ref[...]
-
-    @pl.when((column != 1) & ((column != 0) | (row != 0)))
-    def _():
-        cross_ref[...] = left_ref[...]
-
 
 def third_body(plan_ref, panel_ref, right_ref, left_ref, to_right_ref, to_left_ref, sems):
     @pl.when(plan_ref[0] == 0)
@@ -103,9 +107,8 @@
 
     @pl.when(plan_ref[0] > 0)
     def _():
-        for ref in (to_right_ref, to_left_ref):
-            ref[:256] = right_ref[...]
-            ref[256:] = left_ref[...]
+        to_right_ref[...] = right_ref[...]
+        to_left_ref[...] = left_ref[...]
 
 
 def with_panel(body, out, plan, panel, *received, scratch=()):
@@ -120,7 +123,7 @@
     )(plan, panel, *received)
 
 
-def scatter_columns(panel, owner):
+def scatter_columns(panel, owner, quarter):
     rx = (lax.axis_index("x") - owner // 2) % 4
     ry = (lax.axis_index("yh") - owner % 2) % 2
 
@@ -131,36 +134,41 @@
         return lax.dynamic_slice_in_dim(panel, column(i, j) * 1024, 1024, 1)
 
     places = [column(2, 0), column(0, 1), column(1, 0), column(3, 0), column(0, 0)]
-    plan = jnp.stack([rx, ry, *places, lax.axis_index("core")]).astype(jnp.int32)
+    plan = jnp.stack([rx, ry, *places, quarter]).astype(jnp.int32)
     full, half = shape((512, 1024)), shape((256, 1024))
     to_right = shift_x(block(1, 1), 1)
     to_left = shift_x(block(3, 1), 3)
     across = flip(block(2, 1), "yh")
-    upper, lower, crossing = with_panel(
-        second_body, (half, half, full), plan, panel, to_right, to_left, across,
-        scratch=(pltpu.VMEM((512, 1024), bf16),),
+    lower_right = shift_x(block(1, 0)[256:], 1)
+    lower_left = shift_x(block(3, 0)[256:], 3)
+    crossing = flip(with_panel(cross_body, full, plan, panel, to_right, to_left), "yh")
+    upper, lower = with_panel(
+        far_body, (half, half), plan, panel, across, scratch=(pltpu.VMEM((512, 1024), bf16),)
     )
-    across = flip(crossing, "yh")
     far_right = shift_x(upper, 1)
     far_left = shift_x(lower, 3)
-    near_right, near_left = with_panel(third_body, (full, full), plan, panel, far_right, far_left)
-    return plan, (shift_x(near_right, 1), shift_x(near_left, 3), across)
-
-
-def half_body(core_ref, g_ref, o_ref):
-    pltpu.sync_copy(g_ref.at[:, core_ref[0]], o_ref)
-
-
-def gradient_half(grads, cores):
-    return pl.pallas_call(
-        half_body,
-        out_shape=shape((8, 512, 128)),
+    upper_right, upper_left = with_panel(third_body, (half, half), plan, panel, far_right, far_left)
+    return plan, (shift_x(upper_right, 1), lower_right, shift_x(upper_left, 3), lower_left, crossing)
+
+
+def quarter_body(plan_ref, g_ref, o_ref):
+    pltpu.sync_copy(g_ref.at[:, plan_ref[0]], o_ref)
+
+
+def gradient_quarters(grads, quarter):
+    piece = pl.pallas_call(
+        quarter_body,
+        out_shape=shape((8, 256, 128)),
         in_specs=[pl.BlockSpec(memory_space=pltpu.SMEM), pl.BlockSpec(memory_space=pl.ANY)],
         out_specs=pl.BlockSpec(memory_space=pltpu.VMEM),
-    )(cores, grads.reshape(8, 2, 512, 128))
-
-
-def project_body(plan_ref, panel_ref, g_ref, h_ref, right_ref, left_ref, across_ref, a_ref, o_ref, sems):
+    )(quarter[None].astype(jnp.int32), grads.reshape(8, 4, 256, 128))
+    mine = exchange(piece, GROUP)
+    near = lax.ppermute(mine, "z", [(0, 1), (1, 0), (2, 3), (3, 2)])
+    return mine, near, flip(mine, "core"), flip(near, "core")
+
+
+def project_body(plan_ref, panel_ref, g0_ref, g1_ref, g2_ref, g3_ref, *refs):
+    upper_right, lower_right, upper_left, lower_left, across_ref, a_ref, o_ref, sems = refs
     column, row = plan_ref[0], plan_ref[1]
     straight = row == 0
 
@@ -170,26 +178,33 @@
 
     @pl.when((column == 1) & straight)
     def _():
-        a_ref[...] = right_ref[...]
+        a_ref[:256] = upper_right[...]
+        a_ref[256:] = lower_right[...]
 
     @pl.when((column == 3) & straight)
     def _():
-        a_ref[...] = left_ref[...]
+        a_ref[:256] = upper_left[...]
+        a_ref[256:] = lower_left[...]
 
     @pl.when(column == 2)
     def _():
-        a_ref[:256] = right_ref[:256]
-        a_ref[256:] = left_ref[256:]
+        a_ref[:256] = upper_right[...]
+        a_ref[256:] = upper_left[...]
 
     @pl.when((column != 2) & (row == 1))
     def _():
         a_ref[...] = across_ref[...]
 
-    mine, other = half_of(a_ref, plan_ref[CORE]), half_of(a_ref, 1 - plan_ref[CORE])
+    quarter = plan_ref[QUARTER]
+    half = 2 * (quarter // 2)
+    place = quarter - half
+    columns = (quarter, half + 1 - place, 2 - half + place, 2 - half + 1 - place)
+    parts = [a_ref[:, pl.ds(pl.multiple_of(k * 256, 256), 256)] for k in columns]
     for j in range(4):
-        g = jnp.concatenate([g_ref[2 * j], g_ref[2 * j + 1]], axis=1)
-        h = jnp.concatenate([h_ref[2 * j], h_ref[2 * j + 1]], axis=1)
-        value = jnp.dot(mine, g, preferred_element_type=f32) + jnp.dot(other, h, preferred_element_type=f32)
+        value = jnp.zeros((512, 256), f32)
+        for part, ref in zip(parts, (g0_ref, g1_ref, g2_ref, g3_ref)):
+            rows = jnp.concatenate([ref[2 * j], ref[2 * j + 1]], axis=1)
+            value = value + jnp.dot(part, rows, preferred_element_type=f32)
         o_ref[2 * j] = value[:, :128].astype(bf16)
         o_ref[2 * j + 1] = value[:, 128:].astype(bf16)
 
@@ -303,13 +318,32 @@
         out[...] = ((1.0 + rate) * base.astype(f32) - (rate * (1.0 / 1024.0)) * combined).astype(bf16)
 
 
+def join_body(core_ref, mine_ref, theirs_ref, o_ref, sems):
+    def join(left_ref, right_ref):
+        left = pltpu.make_async_copy(left_ref, o_ref.at[:, 0:512], sems.at[0])
+        right = pltpu.make_async_copy(right_ref, o_ref.at[:, 512:1024], sems.at[1])
+        left.start()
+        right.start()
+        left.wait()
+        right.wait()
+
+    @pl.when(core_ref[0] == 0)
+    def _():
+        join(mine_ref, theirs_ref)
+
+    @pl.when(core_ref[0] == 1)
+    def _():
+        join(theirs_ref, mine_ref)
+
+
 def shards(factors, owner, grads):
     core = lax.axis_index("core")
     cores = core[None].astype(jnp.int32)
-    mine = exchange(gradient_half(grads, cores), GROUP)
-    plan, received = scatter_columns(factors[0], owner[0])
+    quarter = 2 * core + lax.axis_index("z") % 2
+    rows = gradient_quarters(grads, quarter)
+    plan, received = scatter_columns(factors[0], owner[0], quarter)
     tiles = shape((8, 512, 128))
-    own, projected = with_panel(project_body, (shape((512, 1024)), tiles), plan, factors[0], mine, flip(mine, "core"), *received)
+    own, projected = with_panel(project_body, (shape((512, 1024)), tiles), plan, factors[0], *rows, *received)
     projected = exchange(projected, GROUP)
     projected = exchange(call(spread_body, tiles, projected), GROUP)
     given = flip(call(give_body, tiles, cores, own, projected, scalars=1), "core")
@@ -336,9 +370,14 @@
         update_body, (half, half), cores, precond, other, later, near, own, other_own, squares, scalars=1
     )
     theirs = flip(theirs, "core")
-    left = jnp.where(core == 0, mine, theirs)
-    right = jnp.where(core == 0, theirs, mine)
-    return jnp.concatenate([left, right], axis=1)
+    return pl.pallas_call(
+        join_body,
+        out_shape=shape((512, 1024)),
+        in_specs=[pl.BlockSpec(memory_space=pltpu.SMEM)] + [pl.BlockSpec(memory_space=pltpu.VMEM)] * 2,
+        out_specs=pl.BlockSpec(memory_space=pl.ANY),
+        scratch_shapes=[pltpu.SemaphoreType.DMA((2,))],
+        compiler_params=params,
+    )(cores, mine, theirs)
 
 
 def solution(mesh):

time: 238 us -> 236 us (level)
  waiting for transfers between devices: 55.9 us -> 27.5 us
  blocking collectives: 102 us -> 129 us
  starting transfers between devices: 42.7 us -> 46.1 us
    ppermute x7 -> x8, waiting for transfers between devices: 35.7 us -> 6.56 us  [flip(): return lax.ppermute(value, axis, [(0, 1), (1, 0)])]
    all_to_all x4 -> x5, blocking collectives: 71.2 us -> 98.6 us  [exchange(): return lax.all_to_all(tiles, axes, 0, 0, tiled=True)]
    ppermute x7 -> x8, starting transfers between devices: 25.5 us -> 29.5 us  [flip(): return lax.ppermute(value, axis, [(0, 1), (1, 0)])]
    all_to_all x2 -> x1, starting transfers between devices: 7.8 us -> 4.24 us  [exchange(): return lax.all_to_all(tiles, axes, 0, 0, tiled=True)]
    unnamed x18 -> x12, local copies, waits for them, and re-layouts: 8.08 us -> 5.37 us
    ppermute x6 -> x8, starting transfers between devices: 8.73 us -> 10.1 us  [shift_x(): return lax.ppermute(value, 'x', [(i, (i + step) % 4) for i in range(4)])]
    ppermute x6 -> x8, waiting for transfers between devices: 13.7 us -> 13.1 us  [shift_x(): return lax.ppermute(value, 'x', [(i, (i + step) % 4) for i in range(4)])]
    pallas_call x3 -> x4, Pallas kernels: 6.18 us -> 6.42 us  [with_panel(): pl.pallas_call(body, out_shape=out, in_specs=[pl.BlockSpec(memory_space=p...]
  transfers between devices with their start and end apart: 16 -> 19, of which waited for: 7 -> 9; matrix products, arithmetic and copies ran while one was open for 0% -> 1% of each run, Pallas kernels for 4% -> 4%
where the time goes in v3:
time: 236 us
  blocking collectives  129 us (55%)
  starting transfers between devices  46.1 us (20%)
  waiting for transfers between devices  27.5 us (12%)
  Pallas kernels  21.2 us (9%)
  local copies, waits for them, and re-layouts  10.5 us (4%)
    all_to_all x5, blocking collectives, exchange(): return lax.all_to_all(tiles, axes, 0, 0, tiled=True)  98.6 us
    all_to_all x1, blocking collectives, copies_to(): lax.all_to_all(jnp.broadcast_to(value, (8, *value.shape)), axes, 0, 0, ti...  30.6 us
    ppermute x8, starting transfers between devices, flip(): return lax.ppermute(value, axis, [(0, 1), (1, 0)])  29.5 us
    ppermute x8, waiting for transfers between devices, shift_x(): return lax.ppermute(value, 'x', [(i, (i + step) % 4) for i in range(4)])  13.1 us
    pallas_call x8, Pallas kernels, call(): pl.pallas_call(body, out_shape=out, in_specs=specs, out_specs=jax.tree.ma...  11.9 us
    ppermute x8, starting transfers between devices, shift_x(): return lax.ppermute(value, 'x', [(i, (i + step) % 4) for i in range(4)])  10.1 us
    ppermute x8, waiting for transfers between devices, flip(): return lax.ppermute(value, axis, [(0, 1), (1, 0)])  6.56 us
    all_to_all x1, waiting for transfers between devices, exchange(): return lax.all_to_all(tiles, axes, 0, 0, tiled=True)  6.51 us
  transfers between devices with their start and end apart: 19, of which 9 were waited for; matrix products, arithmetic and copies ran while one was open for 1% of the time, Pallas kernels for 4%

profile of v3, /device:TPU:1, one launch (start us, length us, event | category | flops | bytes accessed | tf_op | source)
XLA Modules:
  0.0 235.6 jit_solution(5384774647692909473)
XLA Ops:
  0.8 3.6 %dynamic-slice_bitcast_fusion = (bf16[512,1024]{1,0:T(8,128)(2,1)}, bf16[512,1024]{1,0:T(8,128)(2,1)}, bf16[512,1024]{1,0:T(8,128)(2,1)}) fusion(bf16[1,512,8192]{2,1,0:T(8,128)(2,1)} %param.3, s32[]{:T(128)S(6)} %select_n.138, s32[]{:T(128)S(6)} %select_n.134, s32[]{:T(128)S(6)} %select_n.137), kind=kLoop, calls=%fused_computation | loop fusion | bytes 6291468 | tf_op jit(solution)/shard_map/dynamic_slice | solution.py:134
  4.4 3.7 %collective-permute-start.3 = (bf16[512,1024]{1,0:T(8,128)(2,1)}, bf16[512,1024]{1,0:T(8,128)(2,1)}, u32[]{:S(2)}, u32[]{:S(2)}) collective-permute-start(bf16[512,1024]{1,0:T(8,128)(2,1)} %get-tuple-element.26), channel_id=1, source_target_pairs={{0,16},{16,0},{1,17},{17,1},{2,18},{18,2},{3,19},{19,3},{4,20},{20... | collective-permute-start | bytes 3145736 | tf_op jit(solution)/shard_map/ppermute | solution.py:49
  8.1 2.5 %collective-permute-start.11 = (bf16[512,1024]{1,0:T(8,128)(2,1)}, bf16[512,1024]{1,0:T(8,128)(2,1)S(1)}, u32[]{:S(2)}, u32[]{:S(2)}) collective-permute-start(bf16[512,1024]{1,0:T(8,128)(2,1)} %get-tuple-element.25), channel_id=1, source_target_pairs={{0,96},{32,0},{64,32},{96,64},{1,97},{33,1},{65,33},{97,65},{2,98}... | collective-permute-start | bytes 3145736 | tf_op jit(solution)/shard_map/ppermute | solution.py:45
  12.4 27.7 %all_to_all.35.g0_ref = bf16[8,256,128]{2,1,0:T(8,128)(2,1)S(1)} all-to-all(bf16[8,256,128]{2,1,0:T(8,128)(2,1)} %shard_map.37), channel_id=1, replica_groups=mesh['x'=4,'yh'=2,'yl'=2,'z'=4,'core'=2] {'x','yh'}, dimensions={0} | all-to-all | bytes 1048576 | tf_op jit(solution)/shard_map/all_to_all | solution.py:57
  44.6 2.7 %collective-permute-start.5 = (bf16[256,1024]{1,0:T(8,128)(2,1)S(1)}, bf16[256,1024]{1,0:T(8,128)(2,1)S(1)}, u32[]{:S(2)}, u32[]{:S(2)}) collective-permute-start(bf16[256,1024]{1,0:T(8,128)(2,1)S(1)} %get-tuple-element.16), channel_id=1, source_target_pairs={{0,96},{32,0},{64,32},{96,64},{1,97},{33,1},{65,33},{97,65},{2,98}... | collective-permute-start | bytes 1572872 | tf_op jit(solution)/shard_map/ppermute | solution.py:45
  52.4 3.4 %collective-permute-done.4.right_ref = bf16[256,1024]{1,0:T(8,128)(2,1)S(1)} collective-permute-done((bf16[256,1024]{1,0:T(8,128)(2,1)S(1)}, bf16[256,1024]{1,0:T(8,128)(2,1)S(1)}, u32[]{:S(2)}, u32[]{:S(2)}) %collective-permute-start.4) | collective-permute-done | bytes 524320 | tf_op jit(solution)/shard_map/ppermute | solution.py:45
  55.8 8.2 %collective-permute-start.1 = (bf16[8,256,128]{2,1,0:T(8,128)(2,1)S(1)}, bf16[8,256,128]{2,1,0:T(8,128)(2,1)S(1)}, u32[]{:S(2)}, u32[]{:S(2)}) collective-permute-start(bf16[8,256,128]{2,1,0:T(8,128)(2,1)S(1)} %all_to_all.35.g0_ref), channel_id=1, source_target_pairs={{0,1},{1,0},{2,3},{3,2},{4,5},{5,4},{6,7},{7,6},{8,9},{9,8},{10,11... | collective-permute-start | bytes 1572872 | tf_op jit(solution)/shard_map/ppermute | solution.py:49
  69.5 8.0 %collective-permute-done.6.refs_0_ = bf16[256,1024]{1,0:T(8,128)(2,1)S(1)} collective-permute-done((bf16[256,1024]{1,0:T(8,128)(2,1)S(1)}, bf16[256,1024]{1,0:T(8,128)(2,1)S(1)}, u32[]{:S(2)}, u32[]{:S(2)}) %collective-permute-start.6) | collective-permute-done | bytes 524320 | tf_op jit(solution)/shard_map/ppermute | solution.py:45
  78.8 3.6 %shard_map.41 = (bf16[512,1024]{1,0:T(8,128)(2,1)S(1)}, bf16[8,512,128]{2,1,0:T(8,128)(2,1)}) custom-call(s32[8]{0:T(128)S(1)} %stack.35.plan_ref, bf16[512,8192]{1,0:T(8,128)(2,1)} %bitcast.29, bf16[8,256,128]{2,1,0:T(8,128)(2,1)S(1)} %all_to_all.35.g0_ref, bf16[8,256,128]{2,1,0:T(8,128)(2,1)S(1)} %collective-permute-done.g1_ref, ...), custom_call_target="tpu_custom_call" | custom-call | tf_op jit(solution)/shard_map/pallas_call | solution.py:116
  82.4 17.4 %all_to_all.36.t_ref = bf16[8,512,128]{2,1,0:T(8,128)(2,1)S(1)} all-to-all(bf16[8,512,128]{2,1,0:T(8,128)(2,1)} %get-tuple-element.20), channel_id=1, replica_groups=mesh['x'=4,'yh'=2,'yl'=2,'z'=4,'core'=2] {'x','yh'}, dimensions={0} | all-to-all | bytes 2097152 | tf_op jit(solution)/shard_map/all_to_all | solution.py:57
  100.0 14.1 %all_to_all.37.p_ref = bf16[8,512,128]{2,1,0:T(8,128)(2,1)S(1)} all-to-all(bf16[8,512,128]{2,1,0:T(8,128)(2,1)S(1)} %shard_map.42), channel_id=1, replica_groups=mesh['x'=4,'yh'=2,'yl'=2,'z'=4,'core'=2] {'x','yh'}, dimensions={0} | all-to-all | bytes 2097152 | tf_op jit(solution)/shard_map/all_to_all | solution.py:57
  114.8 9.7 %collective-permute-start.13 = (bf16[8,512,128]{2,1,0:T(8,128)(2,1)S(1)}, bf16[8,512,128]{2,1,0:T(8,128)(2,1)S(1)}, u32[]{:S(2)}, u32[]{:S(2)}) collective-permute-start(bf16[8,512,128]{2,1,0:T(8,128)(2,1)S(1)} %shard_map.43), channel_id=1, source_target_pairs={{0,1},{1,0},{2,3},{3,2},{4,5},{5,4},{6,7},{7,6},{8,9},{9,8},{10,11... | collective-permute-start | bytes 3145736 | tf_op jit(solution)/shard_map/ppermute | solution.py:49
  124.6 2.3 collective-permute-done.13.r_ref
  127.6 18.9 %all_to_all.38.t_ref = bf16[8,512,128]{2,1,0:T(8,128)(2,1)S(1)} all-to-all(bf16[8,512,128]{2,1,0:T(8,128)(2,1)S(1)} %shard_map.44), channel_id=1, replica_groups=mesh['x'=4,'yh'=2,'yl'=2,'z'=4,'core'=2] {'yl','z'}, dimensions={0} | all-to-all | bytes 2097152 | tf_op jit(solution)/shard_map/all_to_all | solution.py:57
  147.5 30.6 %all_to_all.39.q_ref = bf16[8,512,128]{2,1,0:T(8,128)(2,1)S(1)} all-to-all(bf16[8,512,128]{2,1,0:T(8,128)(2,1)S(1)} %broadcast_in_dim.8), channel_id=1, replica_groups=mesh['x'=4,'yh'=2,'yl'=2,'z'=4,'core'=2] {'x','yh'}, dimensions={0} | all-to-all | bytes 2097152 | tf_op jit(solution)/shard_map/all_to_all | solution.py:53
  178.1 2.6 %collective-permute-start.15 = (bf16[8,512,128]{2,1,0:T(8,128)(2,1)S(1)}, bf16[8,512,128]{2,1,0:T(8,128)(2,1)S(1)}, u32[]{:S(2)}, u32[]{:S(2)}) collective-permute-start(bf16[8,512,128]{2,1,0:T(8,128)(2,1)S(1)} %all_to_all.39.q_ref), channel_id=1, source_target_pairs={{0,1},{1,0},{2,3},{3,2},{4,5},{5,4},{6,7},{7,6},{8,9},{9,8},{10,11... | collective-permute-start | bytes 3145736 | tf_op jit(solution)/shard_map/ppermute | solution.py:49
  181.0 2.7 %collective-permute-done.16.b_ref = bf16[512,512]{1,0:T(8,128)(2,1)S(1)} collective-permute-done((bf16[512,512]{1,0:T(8,128)(2,1)S(1)}, bf16[512,512]{1,0:T(8,128)(2,1)S(1)}, u32[]{:S(2)}, u32[]{:S(2)}) %collective-permute-start.16) | collective-permute-done | bytes 524320 | tf_op jit(solution)/shard_map/ppermute | solution.py:49
  183.8 3.1 %shard_map.46 = bf16[8,144,512]{2,1,0:T(8,128)(2,1)S(1)} custom-call(s32[1]{0:T(128)} %bitcast.core_ref, bf16[8,512,128]{2,1,0:T(8,128)(2,1)S(1)} %all_to_all.39.q_ref, bf16[8,512,128]{2,1,0:T(8,128)(2,1)S(1)} %collective-permute-done.15.r_ref, bf16[512,1024]{1,0:T(8,128)(2,1)S(1)} %get-tuple-element.19.a_ref, bf16[512,512]{1,0:T(8,128)(2,1)S(1)} %collective-permute-done.16.b_ref), custom_call_target="tpu_custom_call" | custom-call | tf_op jit(solution)/shard_map/pallas_call | solution.py:22
  186.9 20.6 %all_to_all.40.t_ref = bf16[8,144,512]{2,1,0:T(8,128)(2,1)S(1)} all-to-all(bf16[8,144,512]{2,1,0:T(8,128)(2,1)S(1)} %shard_map.46), channel_id=1, replica_groups=mesh['x'=4,'yh'=2,'yl'=2,'z'=4,'core'=2] {'yl','z'}, dimensions={0} | all-to-all | bytes 2359296 | tf_op jit(solution)/shard_map/all_to_all | solution.py:57
  208.6 4.2 %all-to-all-start.6 = ((bf16[8,128,512]{2,1,0:T(8,128)(2,1)}), bf16[8,128,512]{2,1,0:T(8,128)(2,1)}, u32[]{:S(2)}, u32[]{:S(2)}) async-start(bf16[8,128,512]{2,1,0:T(8,128)(2,1)} %copy-done.4), calls=%async_computation.6 | async-start | bytes 2097152 | tf_op jit(solution)/shard_map/all_to_all | solution.py:57
  213.9 3.7 %shard_map.48.n_ref = f32[2,512,512]{2,1,0:T(8,128)S(1)} custom-call(s32[1]{0:T(128)} %bitcast.core_ref, bf16[8,512,128]{2,1,0:T(8,128)(2,1)S(1)} %all_to_all.39.q_ref, bf16[8,512,128]{2,1,0:T(8,128)(2,1)S(1)} %collective-permute-done.15.r_ref, bf16[512,1024]{1,0:T(8,128)(2,1)S(1)} %get-tuple-element.19.a_ref, bf16[512,512]{1,0:T(8,128)(2,1)S(1)} %copy-done.2), custom_call_target="tpu_custom_call" | custom-call | tf_op jit(solution)/shard_map/pallas_call | solution.py:22
  218.9 6.5 %all-to-all-done.6.s_ref = bf16[8,128,512]{2,1,0:T(8,128)(2,1)} async-done(((bf16[8,128,512]{2,1,0:T(8,128)(2,1)}), bf16[8,128,512]{2,1,0:T(8,128)(2,1)}, u32[]{:S(2)}, u32[]{:S(2)}) %all-to-all-start.6) | async-done | bytes 1048608 | tf_op jit(solution)/shard_map/all_to_all | solution.py:57
  226.5 3.2 %shard_map.49 = (bf16[512,512]{1,0:T(8,128)(2,1)S(1)}, bf16[512,512]{1,0:T(8,128)(2,1)S(1)}) custom-call(s32[1]{0:T(128)} %bitcast.core_ref, bf16[8,512,128]{2,1,0:T(8,128)(2,1)S(1)} %all_to_all.39.q_ref, bf16[8,512,128]{2,1,0:T(8,128)(2,1)S(1)} %collective-permute-done.15.r_ref, bf16[8,128,512]{2,1,0:T(8,128)(2,1)} %all-to-all-done.6.s_ref, ...), custom_call_target="tpu_custom_call" | custom-call | tf_op jit(solution)/shard_map/pallas_call | solution.py:22
  229.7 3.2 %collective-permute-start.17 = (bf16[512,512]{1,0:T(8,128)(2,1)S(1)}, bf16[512,512]{1,0:T(8,128)(2,1)S(1)}, u32[]{:S(2)}, u32[]{:S(2)}) collective-permute-start(bf16[512,512]{1,0:T(8,128)(2,1)S(1)} %get-tuple-element.24), channel_id=1, source_target_pairs={{0,1},{1,0},{2,3},{3,2},{4,5},{5,4},{6,7},{7,6},{8,9},{9,8},{10,11... | collective-permute-start | bytes 1572872 | tf_op jit(solution)/shard_map/ppermute | solution.py:49
  (51 shorter events, 28.2 us)
Async XLA Ops:
  4.4 38.7 %collective-permute-start.3 = (bf16[512,1024]{1,0:T(8,128)(2,1)}, bf16[512,1024]{1,0:T(8,128)(2,1)}, u32[]{:S(2)}, u32[]{:S(2)}) collective-permute-start(bf16[512,1024]{1,0:T(8,128)(2,1)} %get-tuple-element.26), channel_id=1, source_target_pairs={{0,16},{16,0},{1,17},{17,1},{2,18},{18,2},{3,19},{19,3},{4,20},{20... | collective-permute-start | bytes 3145736 | tf_op jit(solution)/shard_map/ppermute | solution.py:49
  8.1 39.1 %collective-permute-start.11 = (bf16[512,1024]{1,0:T(8,128)(2,1)}, bf16[512,1024]{1,0:T(8,128)(2,1)S(1)}, u32[]{:S(2)}, u32[]{:S(2)}) collective-permute-start(bf16[512,1024]{1,0:T(8,128)(2,1)} %get-tuple-element.25), channel_id=1, source_target_pairs={{0,96},{32,0},{64,32},{96,64},{1,97},{33,1},{65,33},{97,65},{2,98}... | collective-permute-start | bytes 3145736 | tf_op jit(solution)/shard_map/ppermute | solution.py:45
  10.6 36.7 %collective-permute-start.10 = (bf16[512,1024]{1,0:T(8,128)(2,1)}, bf16[512,1024]{1,0:T(8,128)(2,1)S(1)}, u32[]{:S(2)}, u32[]{:S(2)}) collective-permute-start(bf16[512,1024]{1,0:T(8,128)(2,1)} %get-tuple-element.27), channel_id=1, source_target_pairs={{0,32},{32,64},{64,96},{96,0},{1,33},{33,65},{65,97},{97,1},{2,34}... | collective-permute-start | bytes 3145736 | tf_op jit(solution)/shard_map/ppermute | solution.py:45
  40.1 10.7 %collective-permute-start = (bf16[8,256,128]{2,1,0:T(8,128)(2,1)S(1)}, bf16[8,256,128]{2,1,0:T(8,128)(2,1)S(1)}, u32[]{:S(2)}, u32[]{:S(2)}) collective-permute-start(bf16[8,256,128]{2,1,0:T(8,128)(2,1)S(1)} %all_to_all.35.g0_ref), channel_id=1, source_target_pairs={{0,2},{2,0},{4,6},{6,4},{1,3},{3,1},{5,7},{7,5},{8,10},{10,8},{12,... | collective-permute-start | bytes 1572872 | tf_op jit(solution)/shard_map/ppermute | solution.py:166
  44.5 11.3 %collective-permute-start.4 = (bf16[256,1024]{1,0:T(8,128)(2,1)S(1)}, bf16[256,1024]{1,0:T(8,128)(2,1)S(1)}, u32[]{:S(2)}, u32[]{:S(2)}) collective-permute-start(bf16[256,1024]{1,0:T(8,128)(2,1)S(1)} %get-tuple-element.15), channel_id=1, source_target_pairs={{0,32},{32,64},{64,96},{96,0},{1,33},{33,65},{65,97},{97,1},{2,34}... | collective-permute-start | bytes 1572872 | tf_op jit(solution)/shard_map/ppermute | solution.py:45
  44.6 19.5 %collective-permute-start.5 = (bf16[256,1024]{1,0:T(8,128)(2,1)S(1)}, bf16[256,1024]{1,0:T(8,128)(2,1)S(1)}, u32[]{:S(2)}, u32[]{:S(2)}) collective-permute-start(bf16[256,1024]{1,0:T(8,128)(2,1)S(1)} %get-tuple-element.16), channel_id=1, source_target_pairs={{0,96},{32,0},{64,32},{96,64},{1,97},{33,1},{65,33},{97,65},{2,98}... | collective-permute-start | bytes 1572872 | tf_op jit(solution)/shard_map/ppermute | solution.py:45
  47.2 18.8 %collective-permute-start.9 = (bf16[256,1024]{1,0:T(8,128)(2,1)S(1)}, bf16[256,1024]{1,0:T(8,128)(2,1)S(1)}, u32[]{:S(2)}, u32[]{:S(2)}) collective-permute-start(bf16[256,1024]{1,0:T(8,128)(2,1)S(1)} %get-tuple-element.28), channel_id=1, source_target_pairs={{0,96},{32,0},{64,32},{96,64},{1,97},{33,1},{65,33},{97,65},{2,98}... | collective-permute-start | bytes 1572872 | tf_op jit(solution)/shard_map/ppermute | solution.py:45
  47.3 20.7 %collective-permute-start.7 = (bf16[256,1024]{1,0:T(8,128)(2,1)S(1)}, bf16[256,1024]{1,0:T(8,128)(2,1)S(1)}, u32[]{:S(2)}, u32[]{:S(2)}) collective-permute-start(bf16[256,1024]{1,0:T(8,128)(2,1)S(1)} %get-tuple-element.29), channel_id=1, source_target_pairs={{0,32},{32,64},{64,96},{96,0},{1,33},{33,65},{65,97},{97,1},{2,34}... | collective-permute-start | bytes 1572872 | tf_op jit(solution)/shard_map/ppermute | solution.py:45
  50.8 27.1 %collective-permute-start.12 = (bf16[512,1024]{1,0:T(8,128)(2,1)S(1)}, bf16[512,1024]{1,0:T(8,128)(2,1)S(1)}, u32[]{:S(2)}, u32[]{:S(2)}) collective-permute-start(bf16[512,1024]{1,0:T(8,128)(2,1)S(1)} %shard_map.40), channel_id=1, source_target_pairs={{0,16},{16,0},{1,17},{17,1},{2,18},{18,2},{3,19},{19,3},{4,20},{20... | collective-permute-start | bytes 3145736 | tf_op jit(solution)/shard_map/ppermute | solution.py:49
  55.8 13.6 %collective-permute-start.1 = (bf16[8,256,128]{2,1,0:T(8,128)(2,1)S(1)}, bf16[8,256,128]{2,1,0:T(8,128)(2,1)S(1)}, u32[]{:S(2)}, u32[]{:S(2)}) collective-permute-start(bf16[8,256,128]{2,1,0:T(8,128)(2,1)S(1)} %all_to_all.35.g0_ref), channel_id=1, source_target_pairs={{0,1},{1,0},{2,3},{3,2},{4,5},{5,4},{6,7},{7,6},{8,9},{9,8},{10,11... | collective-permute-start | bytes 1572872 | tf_op jit(solution)/shard_map/ppermute | solution.py:49
  64.0 5.4 %collective-permute-start.2 = (bf16[8,256,128]{2,1,0:T(8,128)(2,1)S(1)}, bf16[8,256,128]{2,1,0:T(8,128)(2,1)S(1)}, u32[]{:S(2)}, u32[]{:S(2)}) collective-permute-start(bf16[8,256,128]{2,1,0:T(8,128)(2,1)S(1)} %collective-permute-done.g1_ref), channel_id=1, source_target_pairs={{0,1},{1,0},{2,3},{3,2},{4,5},{5,4},{6,7},{7,6},{8,9},{9,8},{10,11... | collective-permute-start | bytes 1572872 | tf_op jit(solution)/shard_map/ppermute | solution.py:49
  66.0 11.4 %collective-permute-start.6 = (bf16[256,1024]{1,0:T(8,128)(2,1)S(1)}, bf16[256,1024]{1,0:T(8,128)(2,1)S(1)}, u32[]{:S(2)}, u32[]{:S(2)}) collective-permute-start(bf16[256,1024]{1,0:T(8,128)(2,1)S(1)} %get-tuple-element.17), channel_id=1, source_target_pairs={{0,32},{32,64},{64,96},{96,0},{1,33},{33,65},{65,97},{97,1},{2,34}... | collective-permute-start | bytes 1572872 | tf_op jit(solution)/shard_map/ppermute | solution.py:45
  68.0 9.8 %collective-permute-start.8 = (bf16[256,1024]{1,0:T(8,128)(2,1)S(1)}, bf16[256,1024]{1,0:T(8,128)(2,1)S(1)}, u32[]{:S(2)}, u32[]{:S(2)}) collective-permute-start(bf16[256,1024]{1,0:T(8,128)(2,1)S(1)} %get-tuple-element.18), channel_id=1, source_target_pairs={{0,96},{32,0},{64,32},{96,64},{1,97},{33,1},{65,33},{97,65},{2,98}... | collective-permute-start | bytes 1572872 | tf_op jit(solution)/shard_map/ppermute | solution.py:45
  114.8 12.0 %collective-permute-start.13 = (bf16[8,512,128]{2,1,0:T(8,128)(2,1)S(1)}, bf16[8,512,128]{2,1,0:T(8,128)(2,1)S(1)}, u32[]{:S(2)}, u32[]{:S(2)}) collective-permute-start(bf16[8,512,128]{2,1,0:T(8,128)(2,1)S(1)} %shard_map.43), channel_id=1, source_target_pairs={{0,1},{1,0},{2,3},{3,2},{4,5},{5,4},{6,7},{7,6},{8,9},{9,8},{10,11... | collective-permute-start | bytes 3145736 | tf_op jit(solution)/shard_map/ppermute | solution.py:49
  146.7 0.7 collective-permute-start.14
  178.1 5.7 %collective-permute-start.15 = (bf16[8,512,128]{2,1,0:T(8,128)(2,1)S(1)}, bf16[8,512,128]{2,1,0:T(8,128)(2,1)S(1)}, u32[]{:S(2)}, u32[]{:S(2)}) collective-permute-start(bf16[8,512,128]{2,1,0:T(8,128)(2,1)S(1)} %all_to_all.39.q_ref), channel_id=1, source_target_pairs={{0,1},{1,0},{2,3},{3,2},{4,5},{5,4},{6,7},{7,6},{8,9},{9,8},{10,11... | collective-permute-start | bytes 3145736 | tf_op jit(solution)/shard_map/ppermute | solution.py:49
  180.7 3.0 %collective-permute-start.16 = (bf16[512,512]{1,0:T(8,128)(2,1)S(1)}, bf16[512,512]{1,0:T(8,128)(2,1)S(1)}, u32[]{:S(2)}, u32[]{:S(2)}) collective-permute-start(bf16[512,512]{1,0:T(8,128)(2,1)S(1)} %constant_dynamic-slice_fusion), channel_id=1, source_target_pairs={{0,1},{1,0},{2,3},{3,2},{4,5},{5,4},{6,7},{7,6},{8,9},{9,8},{10,11... | collective-permute-start | bytes 1572872 | tf_op jit(solution)/shard_map/ppermute | solution.py:49
  183.7 3.2 %copy-start.1 = (bf16[512,512]{1,0:T(8,128)(2,1)}, bf16[512,512]{1,0:T(8,128)(2,1)S(1)}, u32[]{:S(2)}) copy-start(bf16[512,512]{1,0:T(8,128)(2,1)S(1)} %collective-permute-done.16.b_ref) | copy-start | bytes 1572868
  207.6 1.0 copy-start.4
  208.6 16.8 %all-to-all-start.6 = ((bf16[8,128,512]{2,1,0:T(8,128)(2,1)}), bf16[8,128,512]{2,1,0:T(8,128)(2,1)}, u32[]{:S(2)}, u32[]{:S(2)}) async-start(bf16[8,128,512]{2,1,0:T(8,128)(2,1)} %copy-done.4), calls=%async_computation.6 | async-start | bytes 2097152 | tf_op jit(solution)/shard_map/all_to_all | solution.py:57
  212.9 1.0 copy-start.2
  217.6 1.4 copy-start
  225.4 1.0 copy-start.3
  229.7 4.8 %collective-permute-start.17 = (bf16[512,512]{1,0:T(8,128)(2,1)S(1)}, bf16[512,512]{1,0:T(8,128)(2,1)S(1)}, u32[]{:S(2)}, u32[]{:S(2)}) collective-permute-start(bf16[512,512]{1,0:T(8,128)(2,1)S(1)} %get-tuple-element.24), channel_id=1, source_target_pairs={{0,1},{1,0},{2,3},{3,2},{4,5},{5,4},{6,7},{7,6},{8,9},{9,8},{10,11... | collective-permute-start | bytes 1572872 | tf_op jit(solution)/shard_map/ppermute | solution.py:49
  (1 other events, 1.0 us)

commit v4 on v3

--- a/solution.py
+++ b/solution.py
@@ -247,20 +247,30 @@
         o_ref[2 * j + 1] = (value[:, 128:] + r_ref[2 * j + 1].astype(f32)).astype(bf16)
 
 
-def outer_body(core_ref, q_ref, r_ref, a_ref, b_ref, o_ref):
+def squares_of(value):
+    wide = value.astype(f32)
+    return jnp.sum((wide * wide).reshape(64, 8, 2, 128), axis=(0, 2))
+
+
+def outer_own_body(core_ref, q_ref, a_ref, o_ref, s_ref):
     a = half_of(a_ref, core_ref[0])
-    b = b_ref[...]
     squares = jnp.zeros((8, 128), f32)
     for j in range(4):
         q = jnp.concatenate([q_ref[2 * j], q_ref[2 * j + 1]], axis=1)
+        o_ref[256 * j : 256 * j + 256] = contract(q, a, 0, 0)
+        squares = squares + squares_of(q)
+    s_ref[...] = squares
+
+
+def outer_body(p_ref, s_ref, r_ref, b_ref, o_ref):
+    b = b_ref[...]
+    squares = s_ref[...]
+    for j in range(4):
         r = jnp.concatenate([r_ref[2 * j], r_ref[2 * j + 1]], axis=1)
-        value = (contract(q, a, 0, 0) + contract(r, b, 0, 0)).astype(bf16)
+        value = (p_ref[256 * j : 256 * j + 256] + contract(r, b, 0, 0)).astype(bf16)
         o_ref[2 * j, :128] = value[:128]
         o_ref[2 * j + 1, :128] = value[128:]
-        wide = q.astype(f32)
-        squares = squares + jnp.sum((wide * wide).reshape(64, 8, 2, 128), axis=(0, 2))
-        wide = r.astype(f32)
-        squares = squares + jnp.sum((wide * wide).reshape(64, 8, 2, 128), axis=(0, 2))
+        squares = squares + squares_of(r)
     total = jnp.broadcast_to(jnp.sum(squares, axis=(0, 1), keepdims=True), (16, 512))
     top = total.astype(bf16)
     rest = total - top.astype(f32)
@@ -360,7 +370,10 @@
     piece = lax.ppermute(piece, GROUP_CHIP, swap)
     precond = copies_to(piece, GROUP)
     other = flip(precond, "core")
-    products = call(outer_body, shape((8, 144, 512)), cores, precond, other, own, other_own, scalars=1)
+    partial = call(
+        outer_own_body, (shape((1024, 512), f32), shape((8, 128), f32)), cores, precond, own, scalars=1
+    )
+    products = call(outer_body, shape((8, 144, 512)), *partial, other, other_own)
     near = call(near_body, shape((2, 512, 512), f32), cores, precond, other, own, other_own, scalars=1)
     products = exchange(products, CHIP)
     later, squares = call(suffix_body, (shape((8, 128, 512)), shape((8, 128), f32)), products)

time: 236 us -> 235 us (level)
  starting transfers between devices: 46.1 us -> 41.8 us
    ppermute x8, starting transfers between devices: 29.5 us -> 24.5 us  [flip(): return lax.ppermute(value, axis, [(0, 1), (1, 0)])]
    ppermute x8, waiting for transfers between devices: 13.1 us -> 16.8 us  [shift_x(): return lax.ppermute(value, 'x', [(i, (i + step) % 4) for i in range(4)])]
    pallas_call x8 -> x9, Pallas kernels: 11.9 us -> 12 us  [call(): pl.pallas_call(body, out_shape=out, in_specs=specs, out_specs=jax.tree.ma...]
  transfers between devices with their start and end apart: 19 -> 19, of which waited for: 9 -> 8; matrix products, arithmetic and copies ran while one was open for 1% -> 1% of each run, Pallas kernels for 4% -> 4%
where the time goes in v4:
time: 235 us; the launch traced here: 234 us
  blocking collectives  130 us (55%)
  starting transfers between devices  41.8 us (18%)
  waiting for transfers between devices  29.7 us (13%)
  Pallas kernels  21.3 us (9%)
  local copies, waits for them, and re-layouts  10.5 us (4%)
    all_to_all x5, blocking collectives, exchange(): return lax.all_to_all(tiles, axes, 0, 0, tiled=True)  99 us
    all_to_all x1, blocking collectives, copies_to(): lax.all_to_all(jnp.broadcast_to(value, (8, *value.shape)), axes, 0, 0, ti...  30.7 us
    ppermute x8, starting transfers between devices, flip(): return lax.ppermute(value, axis, [(0, 1), (1, 0)])  24.5 us
    ppermute x8, waiting for transfers between devices, shift_x(): return lax.ppermute(value, 'x', [(i, (i + step) % 4) for i in range(4)])  16.8 us
    pallas_call x9, Pallas kernels, call(): pl.pallas_call(body, out_shape=out, in_specs=specs, out_specs=jax.tree.ma...  12 us
    ppermute x8, starting transfers between devices, shift_x(): return lax.ppermute(value, 'x', [(i, (i + step) % 4) for i in range(4)])  10.8 us
    all_to_all x1, waiting for transfers between devices, exchange(): return lax.all_to_all(tiles, axes, 0, 0, tiled=True)  6.47 us
    pallas_call x4, Pallas kernels, with_panel(): pl.pallas_call(body, out_shape=out, in_specs=[pl.BlockSpec(memory_space=p...  6.42 us
  transfers between devices with their start and end apart: 19, of which 8 were waited for; matrix products, arithmetic and copies ran while one was open for 1% of the time, Pallas kernels for 4%

profile of v4, /device:TPU:1, one launch (start us, length us, event | category | flops | bytes accessed | tf_op | source)
XLA Modules:
  0.0 234.0 jit_solution(11891276779608482839)
XLA Ops:
  0.8 3.6 %dynamic-slice_bitcast_fusion = (bf16[512,1024]{1,0:T(8,128)(2,1)}, bf16[512,1024]{1,0:T(8,128)(2,1)}, bf16[512,1024]{1,0:T(8,128)(2,1)}) fusion(bf16[1,512,8192]{2,1,0:T(8,128)(2,1)} %param.3, s32[]{:T(128)S(6)} %select_n.138, s32[]{:T(128)S(6)} %select_n.134, s32[]{:T(128)S(6)} %select_n.137), kind=kLoop, calls=%fused_computation | loop fusion | bytes 6291468 | tf_op jit(solution)/shard_map/dynamic_slice | solution.py:134
  4.4 3.7 %collective-permute-start.3 = (bf16[512,1024]{1,0:T(8,128)(2,1)}, bf16[512,1024]{1,0:T(8,128)(2,1)}, u32[]{:S(2)}, u32[]{:S(2)}) collective-permute-start(bf16[512,1024]{1,0:T(8,128)(2,1)} %get-tuple-element.30), channel_id=1, source_target_pairs={{0,16},{16,0},{1,17},{17,1},{2,18},{18,2},{3,19},{19,3},{4,20},{20... | collective-permute-start | bytes 3145736 | tf_op jit(solution)/shard_map/ppermute | solution.py:49
  12.6 27.2 %all_to_all.35.g0_ref = bf16[8,256,128]{2,1,0:T(8,128)(2,1)S(1)} all-to-all(bf16[8,256,128]{2,1,0:T(8,128)(2,1)} %shard_map.37), channel_id=1, replica_groups=mesh['x'=4,'yh'=2,'yl'=2,'z'=4,'core'=2] {'x','yh'}, dimensions={0} | all-to-all | bytes 1048576 | tf_op jit(solution)/shard_map/all_to_all | solution.py:57
  44.9 2.1 collective-permute-start.5
  47.0 2.7 %collective-permute-start.9 = (bf16[256,1024]{1,0:T(8,128)(2,1)S(1)}, bf16[256,1024]{1,0:T(8,128)(2,1)S(1)}, u32[]{:S(2)}, u32[]{:S(2)}) collective-permute-start(bf16[256,1024]{1,0:T(8,128)(2,1)S(1)} %get-tuple-element.32), channel_id=1, source_target_pairs={{0,96},{32,0},{64,32},{96,64},{1,97},{33,1},{65,33},{97,65},{2,98}... | collective-permute-start | bytes 1572872 | tf_op jit(solution)/shard_map/ppermute | solution.py:45
  53.7 3.1 %collective-permute-done.4.right_ref = bf16[256,1024]{1,0:T(8,128)(2,1)S(1)} collective-permute-done((bf16[256,1024]{1,0:T(8,128)(2,1)S(1)}, bf16[256,1024]{1,0:T(8,128)(2,1)S(1)}, u32[]{:S(2)}, u32[]{:S(2)}) %collective-permute-start.4) | collective-permute-done | bytes 524320 | tf_op jit(solution)/shard_map/ppermute | solution.py:45
  56.8 5.7 %collective-permute-start.1 = (bf16[8,256,128]{2,1,0:T(8,128)(2,1)S(1)}, bf16[8,256,128]{2,1,0:T(8,128)(2,1)S(1)}, u32[]{:S(2)}, u32[]{:S(2)}) collective-permute-start(bf16[8,256,128]{2,1,0:T(8,128)(2,1)S(1)} %all_to_all.35.g0_ref), channel_id=1, source_target_pairs={{0,1},{1,0},{2,3},{3,2},{4,5},{5,4},{6,7},{7,6},{8,9},{9,8},{10,11... | collective-permute-start | bytes 1572872 | tf_op jit(solution)/shard_map/ppermute | solution.py:49
  63.2 4.8 %collective-permute-done.7.refs_1_ = bf16[256,1024]{1,0:T(8,128)(2,1)S(1)} collective-permute-done((bf16[256,1024]{1,0:T(8,128)(2,1)S(1)}, bf16[256,1024]{1,0:T(8,128)(2,1)S(1)}, u32[]{:S(2)}, u32[]{:S(2)}) %collective-permute-start.7) | collective-permute-done | bytes 524320 | tf_op jit(solution)/shard_map/ppermute | solution.py:45
  68.0 2.7 %collective-permute-start.8 = (bf16[256,1024]{1,0:T(8,128)(2,1)S(1)}, bf16[256,1024]{1,0:T(8,128)(2,1)S(1)}, u32[]{:S(2)}, u32[]{:S(2)}) collective-permute-start(bf16[256,1024]{1,0:T(8,128)(2,1)S(1)} %get-tuple-element.20), channel_id=1, source_target_pairs={{0,96},{32,0},{64,32},{96,64},{1,97},{33,1},{65,33},{97,65},{2,98}... | collective-permute-start | bytes 1572872 | tf_op jit(solution)/shard_map/ppermute | solution.py:45
  70.7 8.9 %collective-permute-done.6.refs_0_ = bf16[256,1024]{1,0:T(8,128)(2,1)S(1)} collective-permute-done((bf16[256,1024]{1,0:T(8,128)(2,1)S(1)}, bf16[256,1024]{1,0:T(8,128)(2,1)S(1)}, u32[]{:S(2)}, u32[]{:S(2)}) %collective-permute-start.6) | collective-permute-done | bytes 524320 | tf_op jit(solution)/shard_map/ppermute | solution.py:45
  80.6 3.6 %shard_map.41 = (bf16[512,1024]{1,0:T(8,128)(2,1)S(1)}, bf16[8,512,128]{2,1,0:T(8,128)(2,1)}) custom-call(s32[8]{0:T(128)S(1)} %stack.35.plan_ref, bf16[512,8192]{1,0:T(8,128)(2,1)} %bitcast.29, bf16[8,256,128]{2,1,0:T(8,128)(2,1)S(1)} %all_to_all.35.g0_ref, bf16[8,256,128]{2,1,0:T(8,128)(2,1)S(1)} %collective-permute-done.g1_ref, ...), custom_call_target="tpu_custom_call" | custom-call | tf_op jit(solution)/shard_map/pallas_call | solution.py:116
  84.2 17.5 %all_to_all.36.t_ref = bf16[8,512,128]{2,1,0:T(8,128)(2,1)S(1)} all-to-all(bf16[8,512,128]{2,1,0:T(8,128)(2,1)} %get-tuple-element.22), channel_id=1, replica_groups=mesh['x'=4,'yh'=2,'yl'=2,'z'=4,'core'=2] {'x','yh'}, dimensions={0} | all-to-all | bytes 2097152 | tf_op jit(solution)/shard_map/all_to_all | solution.py:57
  101.9 14.8 %all_to_all.37.p_ref = bf16[8,512,128]{2,1,0:T(8,128)(2,1)S(1)} all-to-all(bf16[8,512,128]{2,1,0:T(8,128)(2,1)S(1)} %shard_map.42), channel_id=1, replica_groups=mesh['x'=4,'yh'=2,'yl'=2,'z'=4,'core'=2] {'x','yh'}, dimensions={0} | all-to-all | bytes 2097152 | tf_op jit(solution)/shard_map/all_to_all | solution.py:57
  117.4 7.0 %collective-permute-start.13 = (bf16[8,512,128]{2,1,0:T(8,128)(2,1)S(1)}, bf16[8,512,128]{2,1,0:T(8,128)(2,1)S(1)}, u32[]{:S(2)}, u32[]{:S(2)}) collective-permute-start(bf16[8,512,128]{2,1,0:T(8,128)(2,1)S(1)} %shard_map.43), channel_id=1, source_target_pairs={{0,1},{1,0},{2,3},{3,2},{4,5},{5,4},{6,7},{7,6},{8,9},{9,8},{10,11... | collective-permute-start | bytes 3145736 | tf_op jit(solution)/shard_map/ppermute | solution.py:49
  124.4 2.3 collective-permute-done.13.r_ref
  127.4 18.9 %all_to_all.38.t_ref = bf16[8,512,128]{2,1,0:T(8,128)(2,1)S(1)} all-to-all(bf16[8,512,128]{2,1,0:T(8,128)(2,1)S(1)} %shard_map.44), channel_id=1, replica_groups=mesh['x'=4,'yh'=2,'yl'=2,'z'=4,'core'=2] {'yl','z'}, dimensions={0} | all-to-all | bytes 2097152 | tf_op jit(solution)/shard_map/all_to_all | solution.py:57
  147.3 30.7 %all_to_all.39.q_ref = bf16[8,512,128]{2,1,0:T(8,128)(2,1)S(1)} all-to-all(bf16[8,512,128]{2,1,0:T(8,128)(2,1)S(1)} %broadcast_in_dim.8), channel_id=1, replica_groups=mesh['x'=4,'yh'=2,'yl'=2,'z'=4,'core'=2] {'x','yh'}, dimensions={0} | all-to-all | bytes 2097152 | tf_op jit(solution)/shard_map/all_to_all | solution.py:53
  178.0 2.6 %collective-permute-start.15 = (bf16[8,512,128]{2,1,0:T(8,128)(2,1)S(1)}, bf16[8,512,128]{2,1,0:T(8,128)(2,1)S(1)}, u32[]{:S(2)}, u32[]{:S(2)}) collective-permute-start(bf16[8,512,128]{2,1,0:T(8,128)(2,1)S(1)} %all_to_all.39.q_ref), channel_id=1, source_target_pairs={{0,1},{1,0},{2,3},{3,2},{4,5},{5,4},{6,7},{7,6},{8,9},{9,8},{10,11... | collective-permute-start | bytes 3145736 | tf_op jit(solution)/shard_map/ppermute | solution.py:49
  185.4 20.5 %all_to_all.40.t_ref = bf16[8,144,512]{2,1,0:T(8,128)(2,1)S(1)} all-to-all(bf16[8,144,512]{2,1,0:T(8,128)(2,1)S(1)} %shard_map.47), channel_id=1, replica_groups=mesh['x'=4,'yh'=2,'yl'=2,'z'=4,'core'=2] {'yl','z'}, dimensions={0} | all-to-all | bytes 2359296 | tf_op jit(solution)/shard_map/all_to_all | solution.py:57
  207.0 4.2 %all-to-all-start.6 = ((bf16[8,128,512]{2,1,0:T(8,128)(2,1)}), bf16[8,128,512]{2,1,0:T(8,128)(2,1)}, u32[]{:S(2)}, u32[]{:S(2)}) async-start(bf16[8,128,512]{2,1,0:T(8,128)(2,1)} %copy-done.4), calls=%async_computation.6 | async-start | bytes 2097152 | tf_op jit(solution)/shard_map/all_to_all | solution.py:57
  212.3 3.7 %shard_map.49.n_ref = f32[2,512,512]{2,1,0:T(8,128)S(1)} custom-call(s32[1]{0:T(128)} %bitcast.core_ref, bf16[8,512,128]{2,1,0:T(8,128)(2,1)S(1)} %all_to_all.39.q_ref, bf16[8,512,128]{2,1,0:T(8,128)(2,1)S(1)} %collective-permute-done.15.r_ref, bf16[512,1024]{1,0:T(8,128)(2,1)S(1)} %get-tuple-element.21.a_ref, bf16[512,512]{1,0:T(8,128)(2,1)S(1)} %copy-done.2), custom_call_target="tpu_custom_call" | custom-call | tf_op jit(solution)/shard_map/pallas_call | solution.py:22
  217.3 6.5 %all-to-all-done.6.s_ref = bf16[8,128,512]{2,1,0:T(8,128)(2,1)} async-done(((bf16[8,128,512]{2,1,0:T(8,128)(2,1)}), bf16[8,128,512]{2,1,0:T(8,128)(2,1)}, u32[]{:S(2)}, u32[]{:S(2)}) %all-to-all-start.6) | async-done | bytes 1048608 | tf_op jit(solution)/shard_map/all_to_all | solution.py:57
  224.9 3.2 %shard_map.50 = (bf16[512,512]{1,0:T(8,128)(2,1)S(1)}, bf16[512,512]{1,0:T(8,128)(2,1)S(1)}) custom-call(s32[1]{0:T(128)} %bitcast.core_ref, bf16[8,512,128]{2,1,0:T(8,128)(2,1)S(1)} %all_to_all.39.q_ref, bf16[8,512,128]{2,1,0:T(8,128)(2,1)S(1)} %collective-permute-done.15.r_ref, bf16[8,128,512]{2,1,0:T(8,128)(2,1)} %all-to-all-done.6.s_ref, ...), custom_call_target="tpu_custom_call" | custom-call | tf_op jit(solution)/shard_map/pallas_call | solution.py:22
  228.1 3.3 %collective-permute-start.17 = (bf16[512,512]{1,0:T(8,128)(2,1)S(1)}, bf16[512,512]{1,0:T(8,128)(2,1)S(1)}, u32[]{:S(2)}, u32[]{:S(2)}) collective-permute-start(bf16[512,512]{1,0:T(8,128)(2,1)S(1)} %get-tuple-element.28), channel_id=1, source_target_pairs={{0,1},{1,0},{2,3},{3,2},{4,5},{5,4},{6,7},{7,6},{8,9},{9,8},{10,11... | collective-permute-start | bytes 1572872 | tf_op jit(solution)/shard_map/ppermute | solution.py:49
  (52 shorter events, 29.6 us)
Async XLA Ops:
  4.4 38.5 %collective-permute-start.3 = (bf16[512,1024]{1,0:T(8,128)(2,1)}, bf16[512,1024]{1,0:T(8,128)(2,1)}, u32[]{:S(2)}, u32[]{:S(2)}) collective-permute-start(bf16[512,1024]{1,0:T(8,128)(2,1)} %get-tuple-element.30), channel_id=1, source_target_pairs={{0,16},{16,0},{1,17},{17,1},{2,18},{18,2},{3,19},{19,3},{4,20},{20... | collective-permute-start | bytes 3145736 | tf_op jit(solution)/shard_map/ppermute | solution.py:49
  8.1 38.9 %collective-permute-start.10 = (bf16[512,1024]{1,0:T(8,128)(2,1)}, bf16[512,1024]{1,0:T(8,128)(2,1)S(1)}, u32[]{:S(2)}, u32[]{:S(2)}) collective-permute-start(bf16[512,1024]{1,0:T(8,128)(2,1)} %get-tuple-element.31), channel_id=1, source_target_pairs={{0,32},{32,64},{64,96},{96,0},{1,33},{33,65},{65,97},{97,1},{2,34}... | collective-permute-start | bytes 3145736 | tf_op jit(solution)/shard_map/ppermute | solution.py:45
  9.3 37.7 %collective-permute-start.11 = (bf16[512,1024]{1,0:T(8,128)(2,1)}, bf16[512,1024]{1,0:T(8,128)(2,1)S(1)}, u32[]{:S(2)}, u32[]{:S(2)}) collective-permute-start(bf16[512,1024]{1,0:T(8,128)(2,1)} %get-tuple-element.29), channel_id=1, source_target_pairs={{0,96},{32,0},{64,32},{96,64},{1,97},{33,1},{65,33},{97,65},{2,98}... | collective-permute-start | bytes 3145736 | tf_op jit(solution)/shard_map/ppermute | solution.py:45
  39.8 11.9 %collective-permute-start = (bf16[8,256,128]{2,1,0:T(8,128)(2,1)S(1)}, bf16[8,256,128]{2,1,0:T(8,128)(2,1)S(1)}, u32[]{:S(2)}, u32[]{:S(2)}) collective-permute-start(bf16[8,256,128]{2,1,0:T(8,128)(2,1)S(1)} %all_to_all.35.g0_ref), channel_id=1, source_target_pairs={{0,2},{2,0},{4,6},{6,4},{1,3},{3,1},{5,7},{7,5},{8,10},{10,8},{12,... | collective-permute-start | bytes 1572872 | tf_op jit(solution)/shard_map/ppermute | solution.py:166
  44.2 12.6 %collective-permute-start.4 = (bf16[256,1024]{1,0:T(8,128)(2,1)S(1)}, bf16[256,1024]{1,0:T(8,128)(2,1)S(1)}, u32[]{:S(2)}, u32[]{:S(2)}) collective-permute-start(bf16[256,1024]{1,0:T(8,128)(2,1)S(1)} %get-tuple-element.17), channel_id=1, source_target_pairs={{0,32},{32,64},{64,96},{96,0},{1,33},{33,65},{65,97},{97,1},{2,34}... | collective-permute-start | bytes 1572872 | tf_op jit(solution)/shard_map/ppermute | solution.py:45
  44.9 17.7 %collective-permute-start.5 = (bf16[256,1024]{1,0:T(8,128)(2,1)S(1)}, bf16[256,1024]{1,0:T(8,128)(2,1)S(1)}, u32[]{:S(2)}, u32[]{:S(2)}) collective-permute-start(bf16[256,1024]{1,0:T(8,128)(2,1)S(1)} %get-tuple-element.18), channel_id=1, source_target_pairs={{0,96},{32,0},{64,32},{96,64},{1,97},{33,1},{65,33},{97,65},{2,98}... | collective-permute-start | bytes 1572872 | tf_op jit(solution)/shard_map/ppermute | solution.py:45
  47.0 21.0 %collective-permute-start.7 = (bf16[256,1024]{1,0:T(8,128)(2,1)S(1)}, bf16[256,1024]{1,0:T(8,128)(2,1)S(1)}, u32[]{:S(2)}, u32[]{:S(2)}) collective-permute-start(bf16[256,1024]{1,0:T(8,128)(2,1)S(1)} %get-tuple-element.33), channel_id=1, source_target_pairs={{0,32},{32,64},{64,96},{96,0},{1,33},{33,65},{65,97},{97,1},{2,34}... | collective-permute-start | bytes 1572872 | tf_op jit(solution)/shard_map/ppermute | solution.py:45
  47.0 21.0 %collective-permute-start.9 = (bf16[256,1024]{1,0:T(8,128)(2,1)S(1)}, bf16[256,1024]{1,0:T(8,128)(2,1)S(1)}, u32[]{:S(2)}, u32[]{:S(2)}) collective-permute-start(bf16[256,1024]{1,0:T(8,128)(2,1)S(1)} %get-tuple-element.32), channel_id=1, source_target_pairs={{0,96},{32,0},{64,32},{96,64},{1,97},{33,1},{65,33},{97,65},{2,98}... | collective-permute-start | bytes 1572872 | tf_op jit(solution)/shard_map/ppermute | solution.py:45
  51.7 27.9 %collective-permute-start.12 = (bf16[512,1024]{1,0:T(8,128)(2,1)S(1)}, bf16[512,1024]{1,0:T(8,128)(2,1)S(1)}, u32[]{:S(2)}, u32[]{:S(2)}) collective-permute-start(bf16[512,1024]{1,0:T(8,128)(2,1)S(1)} %shard_map.40), channel_id=1, source_target_pairs={{0,16},{16,0},{1,17},{17,1},{2,18},{18,2},{3,19},{19,3},{4,20},{20... | collective-permute-start | bytes 3145736 | tf_op jit(solution)/shard_map/ppermute | solution.py:49
  56.8 13.9 %collective-permute-start.1 = (bf16[8,256,128]{2,1,0:T(8,128)(2,1)S(1)}, bf16[8,256,128]{2,1,0:T(8,128)(2,1)S(1)}, u32[]{:S(2)}, u32[]{:S(2)}) collective-permute-start(bf16[8,256,128]{2,1,0:T(8,128)(2,1)S(1)} %all_to_all.35.g0_ref), channel_id=1, source_target_pairs={{0,1},{1,0},{2,3},{3,2},{4,5},{5,4},{6,7},{7,6},{8,9},{9,8},{10,11... | collective-permute-start | bytes 1572872 | tf_op jit(solution)/shard_map/ppermute | solution.py:49
  62.5 8.2 %collective-permute-start.2 = (bf16[8,256,128]{2,1,0:T(8,128)(2,1)S(1)}, bf16[8,256,128]{2,1,0:T(8,128)(2,1)S(1)}, u32[]{:S(2)}, u32[]{:S(2)}) collective-permute-start(bf16[8,256,128]{2,1,0:T(8,128)(2,1)S(1)} %collective-permute-done.g1_ref), channel_id=1, source_target_pairs={{0,1},{1,0},{2,3},{3,2},{4,5},{5,4},{6,7},{7,6},{8,9},{9,8},{10,11... | collective-permute-start | bytes 1572872 | tf_op jit(solution)/shard_map/ppermute | solution.py:49
  68.0 11.6 %collective-permute-start.6 = (bf16[256,1024]{1,0:T(8,128)(2,1)S(1)}, bf16[256,1024]{1,0:T(8,128)(2,1)S(1)}, u32[]{:S(2)}, u32[]{:S(2)}) collective-permute-start(bf16[256,1024]{1,0:T(8,128)(2,1)S(1)} %get-tuple-element.19), channel_id=1, source_target_pairs={{0,32},{32,64},{64,96},{96,0},{1,33},{33,65},{65,97},{97,1},{2,34}... | collective-permute-start | bytes 1572872 | tf_op jit(solution)/shard_map/ppermute | solution.py:45
  68.0 11.6 %collective-permute-start.8 = (bf16[256,1024]{1,0:T(8,128)(2,1)S(1)}, bf16[256,1024]{1,0:T(8,128)(2,1)S(1)}, u32[]{:S(2)}, u32[]{:S(2)}) collective-permute-start(bf16[256,1024]{1,0:T(8,128)(2,1)S(1)} %get-tuple-element.20), channel_id=1, source_target_pairs={{0,96},{32,0},{64,32},{96,64},{1,97},{33,1},{65,33},{97,65},{2,98}... | collective-permute-start | bytes 1572872 | tf_op jit(solution)/shard_map/ppermute | solution.py:45
  117.4 9.3 %collective-permute-start.13 = (bf16[8,512,128]{2,1,0:T(8,128)(2,1)S(1)}, bf16[8,512,128]{2,1,0:T(8,128)(2,1)S(1)}, u32[]{:S(2)}, u32[]{:S(2)}) collective-permute-start(bf16[8,512,128]{2,1,0:T(8,128)(2,1)S(1)} %shard_map.43), channel_id=1, source_target_pairs={{0,1},{1,0},{2,3},{3,2},{4,5},{5,4},{6,7},{7,6},{8,9},{9,8},{10,11... | collective-permute-start | bytes 3145736 | tf_op jit(solution)/shard_map/ppermute | solution.py:49
  146.5 0.7 collective-permute-start.14
  178.0 5.6 %collective-permute-start.15 = (bf16[8,512,128]{2,1,0:T(8,128)(2,1)S(1)}, bf16[8,512,128]{2,1,0:T(8,128)(2,1)S(1)}, u32[]{:S(2)}, u32[]{:S(2)}) collective-permute-start(bf16[8,512,128]{2,1,0:T(8,128)(2,1)S(1)} %all_to_all.39.q_ref), channel_id=1, source_target_pairs={{0,1},{1,0},{2,3},{3,2},{4,5},{5,4},{6,7},{7,6},{8,9},{9,8},{10,11... | collective-permute-start | bytes 3145736 | tf_op jit(solution)/shard_map/ppermute | solution.py:49
  180.6 3.0 %collective-permute-start.16 = (bf16[512,512]{1,0:T(8,128)(2,1)S(1)}, bf16[512,512]{1,0:T(8,128)(2,1)S(1)}, u32[]{:S(2)}, u32[]{:S(2)}) collective-permute-start(bf16[512,512]{1,0:T(8,128)(2,1)S(1)} %constant_dynamic-slice_fusion), channel_id=1, source_target_pairs={{0,1},{1,0},{2,3},{3,2},{4,5},{5,4},{6,7},{7,6},{8,9},{9,8},{10,11... | collective-permute-start | bytes 1572872 | tf_op jit(solution)/shard_map/ppermute | solution.py:49
  183.6 1.8 copy-start.1
  206.0 1.0 copy-start.4
  207.0 16.8 %all-to-all-start.6 = ((bf16[8,128,512]{2,1,0:T(8,128)(2,1)}), bf16[8,128,512]{2,1,0:T(8,128)(2,1)}, u32[]{:S(2)}, u32[]{:S(2)}) async-start(bf16[8,128,512]{2,1,0:T(8,128)(2,1)} %copy-done.4), calls=%async_computation.6 | async-start | bytes 2097152 | tf_op jit(solution)/shard_map/all_to_all | solution.py:57
  211.3 1.0 copy-start.2
  216.0 1.4 copy-start
  223.8 1.0 copy-start.3
  228.1 4.8 %collective-permute-start.17 = (bf16[512,512]{1,0:T(8,128)(2,1)S(1)}, bf16[512,512]{1,0:T(8,128)(2,1)S(1)}, u32[]{:S(2)}, u32[]{:S(2)}) collective-permute-start(bf16[512,512]{1,0:T(8,128)(2,1)S(1)} %get-tuple-element.28), channel_id=1, source_target_pairs={{0,1},{1,0},{2,3},{3,2},{4,5},{5,4},{6,7},{7,6},{8,9},{9,8},{10,11... | collective-permute-start | bytes 1572872 | tf_op jit(solution)/shard_map/ppermute | solution.py:49
  (1 other events, 1.0 us)
